TPU v7x, 32 devices: a whole 2x2x4 slice. The times are simulated.
32 devices in a mesh: group: 8 (over y, x, core), member: 4 (over z).
Axes of the slice: x: 2, y: 2, z: 4, core: 2. Of those that a mesh axis runs over, the one named last changes fastest.
Arguments:
- embeddings: bfloat16 [131072, 256], P(('group', 'member')), may hold values from -64 to 64
- cluster_ids: int32 [131072], P(('group', 'member')), may hold values from 0 to 7, as said below
- centroids: bfloat16 [8, 4096, 256], P('group', 'member'), may hold values from -40 to 40
Outputs:
- new_centroids: float32 [8, 4096, 256], P('group', 'member')
- mass: float32 [8, 4096], P('group', 'member')
Inputs may be any that keep to these rules, and one draw needn't show every extreme that they name: `cluster_ids`: each device's 4096 rows hold exactly 512 rows of every cluster.
All inputs are finite; a program needn't handle non-finite values.
Results may differ from a plain program's by a relative error of at most 0.0006.
Values may be sent and summed in bfloat16 or wider, within the bound.
No kernel may reach another device: no remote copies, remote signals or barrier semaphores. Data moves between devices by JAX's collectives and lax.ppermute only.
A program may use at most 64 MiB of HBM per device.

v0:
```python
import math

import jax
import jax.numpy as jnp
from jax import lax
from jax.sharding import PartitionSpec as P

PRIOR_MASS = 1.0


def local(embeddings, cluster_ids, centroids):
    row_count, feature_dim = embeddings.shape
    cluster_count = lax.axis_size("group")
    member_count = lax.axis_size("member")
    per_target = row_count // (cluster_count * member_count)
    row_order = jnp.argsort(cluster_ids, stable=True)
    packed = embeddings[row_order].reshape(cluster_count, member_count, per_target, feature_dim)
    flat_packed = packed.reshape(cluster_count * member_count, per_target, feature_dim)
    arrived = lax.all_to_all(
        flat_packed, ("group", "member"), split_axis=0, concat_axis=0, tiled=True
    )
    local_rows = arrived.reshape(-1, feature_dim)
    own_centres = centroids[0]
    all_centres = lax.all_gather(own_centres, "member", axis=0, tiled=True)
    centre_norms = jnp.einsum(
        "kd,kd->k", all_centres, all_centres, preferred_element_type=jnp.float32
    )
    factor = 2.0 / math.sqrt(feature_dim)
    total_sub = all_centres.shape[0]
    block_rows = min(512, row_count)
    blocks = local_rows.reshape(row_count // block_rows, block_rows, feature_dim)

    def visit(carry, block_x):
        weighted, total_mass = carry
        scores = lax.dot_general(
            block_x, all_centres, (((1,), (1,)), ((), ())), preferred_element_type=jnp.float32
        )
        logits = (scores - 0.5 * centre_norms) * factor
        weights_block = jax.nn.softmax(logits, axis=-1).astype(jnp.bfloat16)
        weighted = weighted + lax.dot_general(
            weights_block, block_x, (((0,), (0,)), ((), ())), preferred_element_type=jnp.float32
        )
        total_mass = total_mass + jnp.sum(weights_block.astype(jnp.float32), axis=0)
        return ((weighted, total_mass), None)

    start = (jnp.zeros((total_sub, feature_dim), jnp.float32), jnp.zeros((total_sub,), jnp.float32))
    (weighted, total_mass), _ = lax.scan(visit, start, blocks)
    summed, own_mass = (
        lax.psum_scatter(weighted, "member", scatter_dimension=0, tiled=True),
        lax.psum_scatter(total_mass, "member", scatter_dimension=0, tiled=True),
    )
    updated = (summed + PRIOR_MASS * own_centres.astype(jnp.float32)) / (own_mass + PRIOR_MASS)[
        :, None
    ]
    return (updated[None], own_mass[None])


def solution(mesh):
    placed = (P(("group", "member"), None), P(("group", "member")), P("group", "member", None))
    return jax.shard_map(
        local,
        mesh=mesh,
        in_specs=placed,
        out_specs=(P("group", "member", None), P("group", "member")),
        check_vma=False,
    )
```

profile of v0, /device:TPU:0, one launch (start us, length us, event | category | flops | bytes accessed | tf_op | source)
XLA Modules:
  0.0 331.6 jit_solution(7826517180342101466)
XLA Ops:
  7.2 6.6 %sort.17 = (s32[4096]{0:T(1024)}, s32[4096]{0:T(1024)S(1)}) sort(s32[4096]{0:T(1024)} %param.6, s32[4096]{0:T(1024)S(1)} %iota.4), dimensions={0}, to_apply=%region_0.0 | sort | flops 49152 | bytes 65536 | tf_op jit(solution)/shard_map/jit(argsort)/sort | solution.py:16
  13.8 16.9 %gather_fusion = bf16[4096,256]{1,0:T(8,128)(2,1)} fusion(bf16[4096,256]{1,0:T(8,128)(2,1)S(1)} %copy-done, s32[4096]{0:T(1024)S(1)} %fusion.12), kind=kCustom, calls=%fused_computation | custom fusion | bytes 4210688 | tf_op jit(solution)/shard_map/gather | solution.py:17
  30.8 7.5 %all-to-all-start = ((bf16[32,128,256]{2,1,0:T(8,128)(2,1)}), bf16[32,128,256]{2,1,0:T(8,128)(2,1)}, u32[]{:S(2)}, u32[]{:S(2)}) async-start(bf16[32,128,256]{2,1,0:T(8,128)(2,1)} %bitcast.29), calls=%async_computation | async-start | bytes 4194304 | tf_op jit(solution)/shard_map/all_to_all | solution.py:19
  39.0 81.5 %all-gather.3.cloned.1.call-done = bf16[1,4096,256]{2,1,0:T(8,128)(2,1)} async-done(((bf16[1,1024,256]{2,1,0:T(8,128)(2,1)}), bf16[1,4096,256]{2,1,0:T(8,128)(2,1)}) %all-gather.3.cloned.1.call-update) | async-done | bytes 2097168 | tf_op jit(solution)/shard_map/all_gather | solution.py:24
  122.7 124.2 %while.13 = (s32[]{:T(128)}, f32[4096,256]{1,0:T(8,128)}, f32[4096]{0:T(1024)S(1)}, bf16[8,512,256]{2,1,0:T(8,128)(2,1)}, bf16[4096,256]{1,0:T(8,128)(2,1)}, /*index=5*/f32[4096]{0:T(1024)S(1)}, s32[]{:T(128)}, s32[]{:T(128)}) while((s32[]{:T(128)}, f32[4096,256]{1,0:T(8,128)}, f32[4096]{0:T(1024)S(1)}, ...), condition=%wide.region_5.6_spmd.clone, body=%wide.region_1.5_spmd.clone.sunk | while | flops 2178948096 | bytes 44723292 | solution.py:47
  127.8 3.8 %convert_reduce_fusion.2 = (f32[4096]{0:T(1024)S(1)}, bf16[512,4096]{1,0:T(8,128)(2,1)}) fusion(f32[512]{0:T(512)S(1)} %fusion.24, f32[512]{0:T(512)S(1)} %get-tuple-element.120, f32[512,4096]{1,0:T(8,128)S(1)} %get-tuple-element.119, f32[4096]{0:T(1024)S(1)} %broadcast_multiply_fusion.2), kind=kLoop, calls=%fused_computation.1.clone.1 | loop fusion | flops 14675968 | bytes 12619776 | tf_op jit(solution)/shard_map/while/body/eval_jaxpr/reduce_sum | solution.py:43
  131.6 5.5 %convolution_add_fusion.2 = f32[4096,256]{1,0:T(8,128)} fusion(bf16[512,4096]{1,0:T(8,128)(2,1)} %get-tuple-element.121, f32[4096,256]{1,0:T(8,128)} %get-tuple-element.132, pred[]{:T(512)S(6)} %compare.7, bf16[8,512,256]{2,1,0:T(8,128)(2,1)} %get-tuple-element.142, s32[]{:T(128)} %get-tuple-element.131), kind=kOutput, calls=%fused_computation.7.clone.1 | convolution fusion | flops 1075838976 | bytes 12845569 | tf_op jit(solution)/shard_map/while/body/eval_jaxpr/dot_general | solution.py:40
  142.2 3.8 %convert_reduce_fusion.2 = (f32[4096]{0:T(1024)S(1)}, bf16[512,4096]{1,0:T(8,128)(2,1)}) fusion(f32[512]{0:T(512)S(1)} %fusion.24, f32[512]{0:T(512)S(1)} %get-tuple-element.120, f32[512,4096]{1,0:T(8,128)S(1)} %get-tuple-element.119, f32[4096]{0:T(1024)S(1)} %broadcast_multiply_fusion.2), kind=kLoop, calls=%fused_computation.1.clone.1 | loop fusion | flops 14675968 | bytes 12619776 | tf_op jit(solution)/shard_map/while/body/eval_jaxpr/reduce_sum | solution.py:43
  146.0 6.8 %convolution_add_fusion.2 = f32[4096,256]{1,0:T(8,128)} fusion(bf16[512,4096]{1,0:T(8,128)(2,1)} %get-tuple-element.121, f32[4096,256]{1,0:T(8,128)} %get-tuple-element.132, pred[]{:T(512)S(6)} %compare.7, bf16[8,512,256]{2,1,0:T(8,128)(2,1)} %get-tuple-element.142, s32[]{:T(128)} %get-tuple-element.131), kind=kOutput, calls=%fused_computation.7.clone.1 | convolution fusion | flops 1075838976 | bytes 12845569 | tf_op jit(solution)/shard_map/while/body/eval_jaxpr/dot_general | solution.py:40
  157.9 3.8 %convert_reduce_fusion.2 = (f32[4096]{0:T(1024)S(1)}, bf16[512,4096]{1,0:T(8,128)(2,1)}) fusion(f32[512]{0:T(512)S(1)} %fusion.24, f32[512]{0:T(512)S(1)} %get-tuple-element.120, f32[512,4096]{1,0:T(8,128)S(1)} %get-tuple-element.119, f32[4096]{0:T(1024)S(1)} %broadcast_multiply_fusion.2), kind=kLoop, calls=%fused_computation.1.clone.1 | loop fusion | flops 14675968 | bytes 12619776 | tf_op jit(solution)/shard_map/while/body/eval_jaxpr/reduce_sum | solution.py:43
  161.7 6.8 %convolution_add_fusion.2 = f32[4096,256]{1,0:T(8,128)} fusion(bf16[512,4096]{1,0:T(8,128)(2,1)} %get-tuple-element.121, f32[4096,256]{1,0:T(8,128)} %get-tuple-element.132, pred[]{:T(512)S(6)} %compare.7, bf16[8,512,256]{2,1,0:T(8,128)(2,1)} %get-tuple-element.142, s32[]{:T(128)} %get-tuple-element.131), kind=kOutput, calls=%fused_computation.7.clone.1 | convolution fusion | flops 1075838976 | bytes 12845569 | tf_op jit(solution)/shard_map/while/body/eval_jaxpr/dot_general | solution.py:40
  173.6 3.8 %convert_reduce_fusion.2 = (f32[4096]{0:T(1024)S(1)}, bf16[512,4096]{1,0:T(8,128)(2,1)}) fusion(f32[512]{0:T(512)S(1)} %fusion.24, f32[512]{0:T(512)S(1)} %get-tuple-element.120, f32[512,4096]{1,0:T(8,128)S(1)} %get-tuple-element.119, f32[4096]{0:T(1024)S(1)} %broadcast_multiply_fusion.2), kind=kLoop, calls=%fused_computation.1.clone.1 | loop fusion | flops 14675968 | bytes 12619776 | tf_op jit(solution)/shard_map/while/body/eval_jaxpr/reduce_sum | solution.py:43
  177.4 6.8 %convolution_add_fusion.2 = f32[4096,256]{1,0:T(8,128)} fusion(bf16[512,4096]{1,0:T(8,128)(2,1)} %get-tuple-element.121, f32[4096,256]{1,0:T(8,128)} %get-tuple-element.132, pred[]{:T(512)S(6)} %compare.7, bf16[8,512,256]{2,1,0:T(8,128)(2,1)} %get-tuple-element.142, s32[]{:T(128)} %get-tuple-element.131), kind=kOutput, calls=%fused_computation.7.clone.1 | convolution fusion | flops 1075838976 | bytes 12845569 | tf_op jit(solution)/shard_map/while/body/eval_jaxpr/dot_general | solution.py:40
  184.2 3.1 fusion.23
  189.3 3.8 %convert_reduce_fusion.2 = (f32[4096]{0:T(1024)S(1)}, bf16[512,4096]{1,0:T(8,128)(2,1)}) fusion(f32[512]{0:T(512)S(1)} %fusion.24, f32[512]{0:T(512)S(1)} %get-tuple-element.120, f32[512,4096]{1,0:T(8,128)S(1)} %get-tuple-element.119, f32[4096]{0:T(1024)S(1)} %broadcast_multiply_fusion.2), kind=kLoop, calls=%fused_computation.1.clone.1 | loop fusion | flops 14675968 | bytes 12619776 | tf_op jit(solution)/shard_map/while/body/eval_jaxpr/reduce_sum | solution.py:43
  193.0 6.8 %convolution_add_fusion.2 = f32[4096,256]{1,0:T(8,128)} fusion(bf16[512,4096]{1,0:T(8,128)(2,1)} %get-tuple-element.121, f32[4096,256]{1,0:T(8,128)} %get-tuple-element.132, pred[]{:T(512)S(6)} %compare.7, bf16[8,512,256]{2,1,0:T(8,128)(2,1)} %get-tuple-element.142, s32[]{:T(128)} %get-tuple-element.131), kind=kOutput, calls=%fused_computation.7.clone.1 | convolution fusion | flops 1075838976 | bytes 12845569 | tf_op jit(solution)/shard_map/while/body/eval_jaxpr/dot_general | solution.py:40
  205.0 3.8 %convert_reduce_fusion.2 = (f32[4096]{0:T(1024)S(1)}, bf16[512,4096]{1,0:T(8,128)(2,1)}) fusion(f32[512]{0:T(512)S(1)} %fusion.24, f32[512]{0:T(512)S(1)} %get-tuple-element.120, f32[512,4096]{1,0:T(8,128)S(1)} %get-tuple-element.119, f32[4096]{0:T(1024)S(1)} %broadcast_multiply_fusion.2), kind=kLoop, calls=%fused_computation.1.clone.1 | loop fusion | flops 14675968 | bytes 12619776 | tf_op jit(solution)/shard_map/while/body/eval_jaxpr/reduce_sum | solution.py:43
  208.7 6.8 %convolution_add_fusion.2 = f32[4096,256]{1,0:T(8,128)} fusion(bf16[512,4096]{1,0:T(8,128)(2,1)} %get-tuple-element.121, f32[4096,256]{1,0:T(8,128)} %get-tuple-element.132, pred[]{:T(512)S(6)} %compare.7, bf16[8,512,256]{2,1,0:T(8,128)(2,1)} %get-tuple-element.142, s32[]{:T(128)} %get-tuple-element.131), kind=kOutput, calls=%fused_computation.7.clone.1 | convolution fusion | flops 1075838976 | bytes 12845569 | tf_op jit(solution)/shard_map/while/body/eval_jaxpr/dot_general | solution.py:40
  220.6 3.8 %convert_reduce_fusion.2 = (f32[4096]{0:T(1024)S(1)}, bf16[512,4096]{1,0:T(8,128)(2,1)}) fusion(f32[512]{0:T(512)S(1)} %fusion.24, f32[512]{0:T(512)S(1)} %get-tuple-element.120, f32[512,4096]{1,0:T(8,128)S(1)} %get-tuple-element.119, f32[4096]{0:T(1024)S(1)} %broadcast_multiply_fusion.2), kind=kLoop, calls=%fused_computation.1.clone.1 | loop fusion | flops 14675968 | bytes 12619776 | tf_op jit(solution)/shard_map/while/body/eval_jaxpr/reduce_sum | solution.py:43
  224.4 6.8 %convolution_add_fusion.2 = f32[4096,256]{1,0:T(8,128)} fusion(bf16[512,4096]{1,0:T(8,128)(2,1)} %get-tuple-element.121, f32[4096,256]{1,0:T(8,128)} %get-tuple-element.132, pred[]{:T(512)S(6)} %compare.7, bf16[8,512,256]{2,1,0:T(8,128)(2,1)} %get-tuple-element.142, s32[]{:T(128)} %get-tuple-element.131), kind=kOutput, calls=%fused_computation.7.clone.1 | convolution fusion | flops 1075838976 | bytes 12845569 | tf_op jit(solution)/shard_map/while/body/eval_jaxpr/dot_general | solution.py:40
  236.3 3.8 %convert_reduce_fusion.2 = (f32[4096]{0:T(1024)S(1)}, bf16[512,4096]{1,0:T(8,128)(2,1)}) fusion(f32[512]{0:T(512)S(1)} %fusion.24, f32[512]{0:T(512)S(1)} %get-tuple-element.120, f32[512,4096]{1,0:T(8,128)S(1)} %get-tuple-element.119, f32[4096]{0:T(1024)S(1)} %broadcast_multiply_fusion.2), kind=kLoop, calls=%fused_computation.1.clone.1 | loop fusion | flops 14675968 | bytes 12619776 | tf_op jit(solution)/shard_map/while/body/eval_jaxpr/reduce_sum | solution.py:43
  240.1 6.8 %convolution_add_fusion.2 = f32[4096,256]{1,0:T(8,128)} fusion(bf16[512,4096]{1,0:T(8,128)(2,1)} %get-tuple-element.121, f32[4096,256]{1,0:T(8,128)} %get-tuple-element.132, pred[]{:T(512)S(6)} %compare.7, bf16[8,512,256]{2,1,0:T(8,128)(2,1)} %get-tuple-element.142, s32[]{:T(128)} %get-tuple-element.131), kind=kOutput, calls=%fused_computation.7.clone.1 | convolution fusion | flops 1075838976 | bytes 12845569 | tf_op jit(solution)/shard_map/while/body/eval_jaxpr/dot_general | solution.py:40
  248.8 16.4 %all-reduce = f32[4096]{0:T(1024)S(1)} all-reduce(f32[4096]{0:T(1024)S(1)} %get-tuple-element.38), channel_id=4, replica_groups=mesh['group'=8,'member'=4] {'member'}, use_global_device_ids=true, to_apply=%region_7.8.clone | all-reduce | flops 4096 | bytes 32768
  265.8 56.5 %reduce-scatter.2.cloned.1.call-done = f32[1024,256]{1,0:T(8,128)} async-done(((f32[4096,256]{1,0:T(8,128)}), f32[1024,256]{1,0:T(8,128)}) %reduce-scatter.2.cloned.1.call-update) | async-done | bytes 1048592 | tf_op jit(solution)/shard_map/reduce_scatter | solution.py:49
  (50 shorter events, 44.9 us)
Async XLA Ops:
  7.2 6.7 %copy-start = (bf16[4096,256]{1,0:T(8,128)(2,1)S(1)}, bf16[4096,256]{1,0:T(8,128)(2,1)}, u32[]{:S(2)}) copy-start(bf16[4096,256]{1,0:T(8,128)(2,1)} %param.5) | copy-start | bytes 6291460
  30.8 92.0 %all-to-all-start = ((bf16[32,128,256]{2,1,0:T(8,128)(2,1)}), bf16[32,128,256]{2,1,0:T(8,128)(2,1)}, u32[]{:S(2)}, u32[]{:S(2)}) async-start(bf16[32,128,256]{2,1,0:T(8,128)(2,1)} %bitcast.29), calls=%async_computation | async-start | bytes 4194304 | tf_op jit(solution)/shard_map/all_to_all | solution.py:19
  38.2 82.3 %all-gather.3.cloned.1.call-start = ((), (), s32[]{:S(2)}) async-start(), calls=%async_computation.3 | async-start | bytes 2621440 | tf_op jit(solution)/shard_map/all_gather | solution.py:24
  39.0 283.4 %reduce-scatter.2.cloned.1.call-start = ((), (), s32[]{:S(2)}) async-start(), calls=%async_computation.2 | async-start | bytes 5242880 | tf_op jit(solution)/shard_map/reduce_scatter | solution.py:49
  246.9 0.7 copy-start.2
  246.9 75.4 %copy-start.1 = (bf16[1,1024,256]{2,1,0:T(8,128)(2,1)S(1)}, bf16[1,1024,256]{2,1,0:T(8,128)(2,1)}, u32[]{:S(2)}) copy-start(bf16[1,1024,256]{2,1,0:T(8,128)(2,1)} %param.7) | copy-start | bytes 1572868
Sparse Core Ops, SparseCore 0:
  40.6 79.8 all-gather.2
  247.1 75.2 reduce-scatter.1
where the time goes:
time: 332 us
  waiting for transfers between devices  139 us (42%)
  matrix products  77.8 us (23%)
  other arithmetic  58.2 us (18%)
  local copies, waits for them, and re-layouts  18.1 us (5%)
  blocking collectives  16.4 us (5%)
  between operations  14.8 us (4%)
  starting transfers between devices  7.53 us (2%)
    all_gather x1, waiting for transfers between devices, local(): all_centres = lax.all_gather(own_centres, 'member', axis=0, tiled=True)  81.5 us
    reduce_scatter x1, waiting for transfers between devices, local(): lax.psum_scatter(weighted, 'member', scatter_dimension=0, tiled=True)  56.5 us
    dot_general x8, matrix products, visit(): lax.dot_general(weights_block, block_x, (((0,), (0,)), ((), ())), preferr...  53.1 us
    reduce_sum x8, other arithmetic, visit(): total_mass = total_mass + jnp.sum(weights_block.astype(jnp.float32), axis=0)  30.2 us
    dot_general x8, matrix products, visit(): lax.dot_general(block_x, all_centres, (((1,), (1,)), ((), ())), preferred...  24.6 us
    gather x1, local copies, waits for them, and re-layouts, local(): embeddings[row_order]  16.9 us
    unnamed x1, blocking collectives  16.4 us
    reduce_sum x8, other arithmetic, visit(): weights_block = jax.nn.softmax(logits, axis=-1).astype(jnp.bfloat16)  16.1 us
  transfers between devices with their start and end apart: 3, of which 2 were waited for; matrix products, arithmetic and copies ran while one was open for 1% of the time, Pallas kernels for 0%

commit v1 on v0

v1 whole, which is shorter than its diff:
```python
import functools
import math

import jax
import jax.numpy as jnp
from jax import lax
from jax.experimental import pallas as pl
from jax.experimental.pallas import tpu as pltpu
from jax.sharding import PartitionSpec as P

PRIOR_MASS = 1.0
LOG2E = 1.4426950408889634
SEND_SCALE = 512.0
MASS_SCALE = 8.0
PAD = 16
NT = (((1,), (1,)), ((), ()))


def full(shape):
    return pl.BlockSpec(shape, lambda *_: (0,) * len(shape))


def regroup_kernel(ids_ref, x_ref, out_ref, dest_ref):
    lines, width = ids_ref.shape
    clusters = pl.num_programs(0)
    per = out_ref.shape[1]

    @pl.when(pl.program_id(0) == 0)
    def _():
        ids = ids_ref[...]
        upto = (
            lax.broadcasted_iota(jnp.int32, (width, width), 0)
            <= lax.broadcasted_iota(jnp.int32, (width, width), 1)
        )
        upto = jnp.where(upto, 1.0, 0.0).astype(jnp.bfloat16)
        before = (
            lax.broadcasted_iota(jnp.int32, (lines, lines), 1)
            < lax.broadcasted_iota(jnp.int32, (lines, lines), 0)
        )
        before = jnp.where(before, 1.0, 0.0).astype(jnp.bfloat16)
        ones = jnp.ones((width, width), jnp.bfloat16)
        dest = jnp.zeros((lines, width), jnp.float32)
        for c in range(clusters):
            mask = ids == c
            hot = jnp.where(mask, 1.0, 0.0).astype(jnp.bfloat16)
            within = jnp.dot(hot, upto, preferred_element_type=jnp.float32)
            total = jnp.dot(hot, ones, preferred_element_type=jnp.float32)
            ahead = jnp.dot(
                before, total.astype(jnp.bfloat16), preferred_element_type=jnp.float32
            )
            dest = jnp.where(mask, within + ahead + float(c * per - 1), dest)
        dest_ref[...] = dest.astype(jnp.int32)

    first = pl.program_id(0) * per
    slot = lax.broadcasted_iota(jnp.int32, (per, width), 0) + first
    total = jnp.zeros((per, x_ref.shape[1]), jnp.float32)
    for j in range(lines):
        hot = jnp.where(dest_ref[j : j + 1, :] == slot, 1.0, 0.0).astype(jnp.bfloat16)
        total = total + jnp.dot(
            hot, x_ref[j * width : (j + 1) * width, :], preferred_element_type=jnp.float32
        )
    out_ref[0] = total.astype(out_ref.dtype)


def regroup(ids, x, clusters):
    rows, dim = x.shape
    width = 256
    lines = rows // width
    per = rows // clusters
    return pl.pallas_call(
        regroup_kernel,
        grid=(clusters,),
        in_specs=[full((lines, width)), full((rows, dim))],
        out_specs=pl.BlockSpec((1, per, dim), lambda c: (c, 0, 0)),
        out_shape=jax.ShapeDtypeStruct((clusters, per, dim), x.dtype),
        scratch_shapes=[pltpu.VMEM((lines, width), jnp.int32)],
        cost_estimate=pl.CostEstimate(
            flops=2 * rows * rows * dim, bytes_accessed=4 * rows * dim, transcendentals=0
        ),
        name="regroup",
    )(ids.reshape(lines, width), x)


def half_norms(c, factor):
    sq = c.astype(jnp.float32)
    sq = sq * sq
    high = sq.astype(jnp.bfloat16)
    low = (sq - high.astype(jnp.float32)).astype(jnp.bfloat16)
    ones = jnp.ones((8, c.shape[1]), jnp.bfloat16)
    total = lax.dot_general(ones, high, NT, preferred_element_type=jnp.float32)
    total = total + lax.dot_general(ones, low, NT, preferred_element_type=jnp.float32)
    return total[0:1] * (0.5 * factor)


def logits_of(x, c, h, factor):
    s = lax.dot_general(x, c, NT, preferred_element_type=jnp.float32)
    return s * factor - h


def stats_kernel(factor, lanes, members, x_ref, *refs):
    c_refs = refs[:members]
    m_ref, inv_ref, h_ref, l_ref = refs[members:]
    rows = x_ref.shape[0]
    sub = c_refs[0].shape[0]

    @pl.when(pl.program_id(0) == 0)
    def _():
        for j in range(members):
            h_ref[:, j * sub : (j + 1) * sub] = half_norms(c_refs[j][...], factor)

    x = x_ref[...]
    top = None
    for j in range(members):
        for k in range(0, sub, lanes):
            at = j * sub + k
            l = logits_of(x, c_refs[j][k : k + lanes, :], h_ref[:, at : at + lanes], factor)
            l_ref[:, at : at + lanes] = l
            for q in range(0, lanes, 128):
                part = l[:, q : q + 128]
                top = part if top is None else jnp.maximum(top, part)
    top = jnp.max(top, axis=1, keepdims=True)
    top = jnp.broadcast_to(top, (rows, 128))
    total = jnp.zeros((rows, 128), jnp.float32)
    for at in range(0, members * sub, 128):
        total = total + jnp.exp(l_ref[:, at : at + 128] - top)
    total = jnp.broadcast_to(jnp.sum(total, axis=1, keepdims=True), (rows, 128))
    m_ref[...] = top
    inv_ref[...] = 1.0 / total


def stats(x, shards, factor, tile):
    rows, dim = x.shape
    members, sub = len(shards), shards[0].shape[0]
    lanes = min(256, sub)
    wide = pl.BlockSpec((tile, 128), lambda i: (i, 0))
    return pl.pallas_call(
        functools.partial(stats_kernel, factor, lanes, members),
        grid=(rows // tile,),
        in_specs=[pl.BlockSpec((tile, dim), lambda i: (i, 0))] + [full((sub, dim))] * members,
        out_specs=[wide, wide],
        out_shape=[jax.ShapeDtypeStruct((rows, 128), jnp.float32)] * 2,
        scratch_shapes=[
            pltpu.VMEM((1, members * sub), jnp.float32),
            pltpu.VMEM((tile, members * sub), jnp.float32),
        ],
        cost_estimate=pl.CostEstimate(
            flops=2 * rows * members * sub * dim,
            bytes_accessed=2 * dim * (rows + members * sub) + 1024 * rows,
            transcendentals=rows * members * sub,
        ),
        name="stats",
    )(x, *shards)


def weigh_kernel(factor, lanes, send, x_ref, m_ref, inv_ref, c_ref, *refs):
    if send:
        out_ref, h_ref, xt_ref, acc_ref = refs
    else:
        acc_ref, h_ref, xt_ref = refs
    rows, dim = x_ref.shape
    sub = c_ref.shape[0]

    @pl.when(pl.program_id(0) == 0)
    def _():
        h_ref[...] = half_norms(c_ref[...], factor)
        xt_ref[dim:, :] = jnp.ones((PAD, rows), jnp.bfloat16)
        acc_ref[...] = jnp.zeros_like(acc_ref)

    x = x_ref[...]
    xt_ref[:dim, :] = x.T
    xt = xt_ref[...]
    m = jnp.concatenate([m_ref[...]] * (lanes // 128), axis=1)
    inv = jnp.concatenate([inv_ref[...]] * (lanes // 128), axis=1)
    for k in range(0, sub, lanes):
        l = logits_of(x, c_ref[k : k + lanes, :], h_ref[:, k : k + lanes], factor)
        r = (jnp.exp(l - m) * inv).astype(jnp.bfloat16)
        acc_ref[:, k : k + lanes] += jnp.dot(xt, r, preferred_element_type=jnp.float32)

    if send:

        @pl.when(pl.program_id(0) == pl.num_programs(0) - 1)
        def _():
            mass = acc_ref[dim : dim + 1, :]
            scale = SEND_SCALE / jnp.maximum(mass, 1e-30)
            out_ref[:dim, :] = acc_ref[:dim, :] * scale
            mass = mass * MASS_SCALE
            parts = []
            for _ in range(3):
                part = mass.astype(jnp.bfloat16).astype(jnp.float32)
                parts.append(part)
                mass = mass - part
            rest = jnp.zeros((PAD - 3, sub), jnp.float32)
            out_ref[dim:, :] = jnp.concatenate(parts + [rest], axis=0)


def weigh(x, m, inv, c, factor, tile, send):
    rows, dim = x.shape
    sub = c.shape[0]
    lanes = min(256, sub)
    wide = pl.BlockSpec((tile, 128), lambda i: (i, 0))
    acc = (dim + PAD, sub)
    scratch = [pltpu.VMEM((1, sub), jnp.float32), pltpu.VMEM((dim + PAD, tile), jnp.bfloat16)]
    if send:
        scratch.append(pltpu.VMEM(acc, jnp.float32))
    return pl.pallas_call(
        functools.partial(weigh_kernel, factor, lanes, send),
        grid=(rows // tile,),
        in_specs=[pl.BlockSpec((tile, dim), lambda i: (i, 0)), wide, wide, full((sub, dim))],
        out_specs=full(acc),
        out_shape=jax.ShapeDtypeStruct(acc, jnp.float32),
        scratch_shapes=scratch,
        cost_estimate=pl.CostEstimate(
            flops=4 * rows * sub * dim,
            bytes_accessed=2 * dim * (rows + sub) + 1024 * rows,
            transcendentals=rows * sub,
        ),
        name="weigh",
    )(x, m, inv, c)


def finish_kernel(own_ref, c_ref, *refs):
    arrived, out_ref, mass_ref = refs[:-2], refs[-2], refs[-1]
    dim = c_ref.shape[1]
    total = own_ref[:dim, :]
    mass = own_ref[dim : dim + 1, :]
    for ref in arrived:
        parts = ref[dim:, :]
        part = (parts[0:1] + parts[1:2] + parts[2:3]) * (1.0 / MASS_SCALE)
        total = total + ref[:dim, :] * (part * (1.0 / SEND_SCALE))
        mass = mass + part
    mass_ref[...] = mass
    prior = PRIOR_MASS * c_ref[...].astype(jnp.float32)
    inv = 1.0 / (mass + PRIOR_MASS)
    out_ref[...] = (total * inv).T + prior * jnp.broadcast_to(inv, (8, inv.shape[1])).T[:, 0:1]


def finish(own, c, arrived):
    sub, dim = c.shape
    return pl.pallas_call(
        finish_kernel,
        out_shape=[
            jax.ShapeDtypeStruct((sub, dim), jnp.float32),
            jax.ShapeDtypeStruct((1, sub), jnp.float32),
        ],
        name="finish",
    )(own, c, *arrived)


def local(embeddings, cluster_ids, centroids):
    rows, dim = embeddings.shape
    clusters = lax.axis_size("group")
    members = lax.axis_size("member")
    factor = 2.0 / math.sqrt(dim)
    own = centroids[0]

    def rotate(value, step):
        return lax.ppermute(
            value, "member", [(i, (i + step) % members) for i in range(members)]
        )

    order = sorted(range(1, members), key=lambda d: abs(d - members / 2))
    arrived = {d: rotate(own, d) for d in order}
    packed = regroup(cluster_ids, embeddings, clusters)
    x = lax.all_to_all(packed, "group", split_axis=0, concat_axis=0, tiled=True)
    x = x.reshape(rows, dim)
    m, inv = stats(x, [own] + [arrived[d] for d in order], factor, min(256, rows))
    tile = min(512, rows)
    back = []
    for d in order:
        partial = weigh(x, m, inv, arrived[d], factor, tile, True).astype(jnp.float16)
        back.append(rotate(partial, -d).astype(jnp.float32))
    mine = weigh(x, m, inv, own, factor, tile, False)
    updated, mass = finish(mine, own, back)
    return updated[None], mass


def solution(mesh):
    placed = (P(("group", "member"), None), P(("group", "member")), P("group", "member", None))
    return jax.shard_map(
        local,
        mesh=mesh,
        in_specs=placed,
        out_specs=(P("group", "member", None), P("group", "member")),
        check_vma=False,
    )
```

time: 332 us -> 175 us (0.53)
  Pallas kernels: 0 us -> 95.3 us
  waiting for transfers between devices: 139 us -> 53.6 us
  matrix products: 77.8 us -> 0 us
  other arithmetic: 58.2 us -> 7.24 us
  blocking collectives: 16.4 us -> 0 us
  local copies, waits for them, and re-layouts: 18.1 us -> 3.65 us
  between operations: 14.8 us -> 0.69 us
  starting transfers between devices: 7.53 us -> 14 us
    pallas_call x0 -> x7, Pallas kernels: none -> 95.3 us  [the longest x4 48.9 us: weigh(): pl.pallas_call(functools.partial(weigh_kernel, factor, lanes, send), grid...]
    all_gather x1 -> x0, waiting for transfers between devices: 81.5 us -> none  [local(): all_centres = lax.all_gather(own_centres, 'member', axis=0, tiled=True)]
    dot_general x16 -> x0, matrix products: 77.8 us -> none  [the longest x8 53.1 us: visit(): lax.dot_general(weights_block, block_x, (((0,), (0,)), ((), ())), preferr...]
    reduce_scatter x1 -> x0, waiting for transfers between devices: 56.5 us -> none  [local(): lax.psum_scatter(weighted, 'member', scatter_dimension=0, tiled=True)]
    ppermute x0 -> x6, waiting for transfers between devices: none -> 53.6 us  [rotate(): lax.ppermute(value, 'member', [(i, (i + step) % members) for i in range(m...]
    reduce_sum x16 -> x0, other arithmetic: 46.3 us -> none  [the longest x8 30.2 us: visit(): total_mass = total_mass + jnp.sum(weights_block.astype(jnp.float32), axis=0)]
    gather x1 -> x0, local copies, waits for them, and re-layouts: 16.9 us -> none  [local(): embeddings[row_order]]
    unnamed x1 -> x0, blocking collectives: 16.4 us -> none
  transfers between devices with their start and end apart: 3 -> 7, of which waited for: 2 -> 4; matrix products, arithmetic and copies ran while one was open for 1% -> 3% of each run, Pallas kernels for 0% -> 21%
where the time goes in v1:
time: 175 us; the launch traced here: 174 us
  Pallas kernels  95.3 us (54%)
  waiting for transfers between devices  53.6 us (31%)
  starting transfers between devices  14 us (8%)
  other arithmetic  7.24 us (4%)
  local copies, waits for them, and re-layouts  3.65 us (2%)
    ppermute x6, waiting for transfers between devices, rotate(): lax.ppermute(value, 'member', [(i, (i + step) % members) for i in range(m...  53.6 us
    pallas_call x4, Pallas kernels, weigh(): pl.pallas_call(functools.partial(weigh_kernel, factor, lanes, send), grid...  48.9 us
    pallas_call x1, Pallas kernels, stats(): pl.pallas_call(functools.partial(stats_kernel, factor, lanes, members), g...  28.8 us
    pallas_call x1, Pallas kernels, regroup(): pl.pallas_call(regroup_kernel, grid=(clusters,), in_specs=[full((lines, w...  13.5 us
    ppermute x6, starting transfers between devices, rotate(): lax.ppermute(value, 'member', [(i, (i + step) % members) for i in range(m...  8.64 us
    all_to_all x1, starting transfers between devices, local(): x = lax.all_to_all(packed, 'group', split_axis=0, concat_axis=0, tiled=True)  5.33 us
    pallas_call x1, Pallas kernels, finish(): pl.pallas_call(finish_kernel, out_shape=[jax.ShapeDtypeStruct((sub, dim),...  4.08 us
    convert_element_type x3, other arithmetic, local(): weigh(x, m, inv, arrived[d], factor, tile, True).astype(jnp.float16)  3.98 us
  transfers between devices with their start and end apart: 7, of which 4 were waited for; matrix products, arithmetic and copies ran while one was open for 3% of the time, Pallas kernels for 21%

profile of v1, /device:TPU:0, one launch (start us, length us, event | category | flops | bytes accessed | tf_op | source)
XLA Modules:
  0.0 174.4 jit_solution(14807342250704013723)
XLA Ops:
  0.6 1.3 reshape.10.ids_ref
  2.0 13.5 %regroup.1 = bf16[8,512,256]{2,1,0:T(8,128)(2,1)} custom-call(s32[16,256]{1,0:T(8,128)} %reshape.10.ids_ref, bf16[4096,256]{1,0:T(8,128)(2,1)} %x_ref.1), custom_call_target="tpu_custom_call" | custom-call | flops 8589934592 | bytes 4194304 | tf_op jit(solution)/shard_map/regroup/pallas_call | solution.py:70
  15.4 5.3 %all-to-all-start = ((bf16[8,512,256]{2,1,0:T(8,128)(2,1)}), bf16[8,512,256]{2,1,0:T(8,128)(2,1)S(1)}, u32[]{:S(2)}, u32[]{:S(2)}) async-start(bf16[8,512,256]{2,1,0:T(8,128)(2,1)} %regroup.1), calls=%async_computation | async-start | bytes 4194304 | tf_op jit(solution)/shard_map/all_to_all | solution.py:264
  20.8 3.7 %collective-permute-start.2 = (bf16[1024,256]{1,0:T(8,128)(2,1)S(1)}, bf16[1024,256]{1,0:T(8,128)(2,1)S(1)}, u32[]{:S(2)}, u32[]{:S(2)}) collective-permute-start(bf16[1024,256]{1,0:T(8,128)(2,1)S(1)} %bitcast.11), channel_id=1, source_target_pairs={{0,3},{1,0},{2,1},{3,2},{4,7},{5,4},{6,5},{7,6},{8,11},{9,8},{10,9... | collective-permute-start | bytes 1572872 | tf_op jit(solution)/shard_map/ppermute | solution.py:257
  24.4 1.0 collective-permute-start
  25.4 11.3 %collective-permute-done.2.refs_3_.c_ref = bf16[1024,256]{1,0:T(8,128)(2,1)S(1)} collective-permute-done((bf16[1024,256]{1,0:T(8,128)(2,1)S(1)}, bf16[1024,256]{1,0:T(8,128)(2,1)S(1)}, u32[]{:S(2)}, u32[]{:S(2)}) %collective-permute-start.2) | collective-permute-done | bytes 524320 | tf_op jit(solution)/shard_map/ppermute | solution.py:257
  36.8 12.2 %collective-permute-done.1.refs_2_.c_ref = bf16[1024,256]{1,0:T(8,128)(2,1)S(1)} collective-permute-done((bf16[1024,256]{1,0:T(8,128)(2,1)S(1)}, bf16[1024,256]{1,0:T(8,128)(2,1)S(1)}, u32[]{:S(2)}, u32[]{:S(2)}) %collective-permute-start.1) | collective-permute-done | bytes 524320 | tf_op jit(solution)/shard_map/ppermute | solution.py:257
  49.0 0.8 copy-done.3
  49.8 20.0 %collective-permute-done.refs_1_.c_ref = bf16[1024,256]{1,0:T(8,128)(2,1)S(1)} collective-permute-done((bf16[1024,256]{1,0:T(8,128)(2,1)S(1)}, bf16[1024,256]{1,0:T(8,128)(2,1)S(1)}, u32[]{:S(2)}, u32[]{:S(2)}) %collective-permute-start) | collective-permute-done | bytes 524320 | tf_op jit(solution)/shard_map/ppermute | solution.py:257
  69.8 0.8 copy-done.2
  71.3 28.8 %stats.1 = (f32[4096,128]{1,0:T(8,128)}, f32[4096,128]{1,0:T(8,128)}) custom-call(bf16[4096,256]{1,0:T(8,128)(2,1)} %bitcast.3, bf16[1024,256]{1,0:T(8,128)(2,1)} %bitcast.8, bf16[1024,256]{1,0:T(8,128)(2,1)} %copy-done.2, bf16[1024,256]{1,0:T(8,128)(2,1)} %copy-done.3, bf16[1024,256]{1,0:T(8,128)(2,1)} %copy-done.4), custom_call_target="tpu_custom_call" | custom-call | flops 8589934592 | bytes 8388608 | tf_op jit(solution)/shard_map/stats/pallas_call | solution.py:136
  100.2 12.3 %weigh.7 = f32[272,1024]{1,0:T(8,128)} custom-call(bf16[4096,256]{1,0:T(8,128)(2,1)} %bitcast.4, f32[4096,128]{1,0:T(8,128)} %get-tuple-element.6.m_ref, f32[4096,128]{1,0:T(8,128)} %get-tuple-element.7.inv_ref, bf16[1024,256]{1,0:T(8,128)(2,1)} %copy-done.4), custom_call_target="tpu_custom_call" | custom-call | flops 4294967296 | bytes 6815744 | tf_op jit(solution)/shard_map/weigh/pallas_call | solution.py:205
  112.4 1.3 convert_element_type.22
  113.8 12.3 %weigh.6 = f32[272,1024]{1,0:T(8,128)} custom-call(bf16[4096,256]{1,0:T(8,128)(2,1)} %bitcast.5, f32[4096,128]{1,0:T(8,128)} %get-tuple-element.6.m_ref, f32[4096,128]{1,0:T(8,128)} %get-tuple-element.7.inv_ref, bf16[1024,256]{1,0:T(8,128)(2,1)} %copy-done.3), custom_call_target="tpu_custom_call" | custom-call | flops 4294967296 | bytes 6815744 | tf_op jit(solution)/shard_map/weigh/pallas_call | solution.py:205
  126.1 1.3 convert_element_type.20
  127.4 3.8 %collective-permute-start.4 = (f16[272,1024]{1,0:T(8,128)(2,1)S(1)}, f16[272,1024]{1,0:T(8,128)(2,1)S(1)}, u32[]{:S(2)}, u32[]{:S(2)}) collective-permute-start(f16[272,1024]{1,0:T(8,128)(2,1)S(1)} %convert_element_type.20), channel_id=1, source_target_pairs={{0,3},{1,0},{2,1},{3,2},{4,7},{5,4},{6,5},{7,6},{8,11},{9,8},{10,9... | collective-permute-start | bytes 1671176 | tf_op jit(solution)/shard_map/ppermute | solution.py:257
  131.3 12.2 %weigh.5 = f32[272,1024]{1,0:T(8,128)} custom-call(bf16[4096,256]{1,0:T(8,128)(2,1)} %bitcast.6, f32[4096,128]{1,0:T(8,128)} %get-tuple-element.6.m_ref, f32[4096,128]{1,0:T(8,128)} %get-tuple-element.7.inv_ref, bf16[1024,256]{1,0:T(8,128)(2,1)} %copy-done.2), custom_call_target="tpu_custom_call" | custom-call | flops 4294967296 | bytes 6815744 | tf_op jit(solution)/shard_map/weigh/pallas_call | solution.py:205
  143.5 1.3 convert_element_type.18
  144.9 12.2 %weigh.4.own_ref = f32[272,1024]{1,0:T(8,128)} custom-call(bf16[4096,256]{1,0:T(8,128)(2,1)} %bitcast.7, f32[4096,128]{1,0:T(8,128)} %get-tuple-element.6.m_ref, f32[4096,128]{1,0:T(8,128)} %get-tuple-element.7.inv_ref, bf16[1024,256]{1,0:T(8,128)(2,1)} %bitcast.9), custom_call_target="tpu_custom_call" | custom-call | flops 4294967296 | bytes 6815744 | tf_op jit(solution)/shard_map/weigh/pallas_call | solution.py:205
  157.1 1.1 convert_element_type.23.refs_2_
  158.2 1.1 convert_element_type.21.refs_1_
  159.3 10.0 %collective-permute-done.3 = f16[272,1024]{1,0:T(8,128)(2,1)S(1)} collective-permute-done((f16[272,1024]{1,0:T(8,128)(2,1)S(1)}, f16[272,1024]{1,0:T(8,128)(2,1)S(1)}, u32[]{:S(2)}, u32[]{:S(2)}) %collective-permute-start.3) | collective-permute-done | bytes 557088 | tf_op jit(solution)/shard_map/ppermute | solution.py:257
  169.3 1.1 convert_element_type.19.refs_0_
  170.4 4.1 %finish.1 = (f32[1024,256]{1,0:T(8,128)}, f32[1,1024]{1,0:T(1,128)}) custom-call(f32[272,1024]{1,0:T(8,128)} %weigh.4.own_ref, bf16[1024,256]{1,0:T(8,128)(2,1)} %bitcast.10, f32[272,1024]{1,0:T(8,128)} %convert_element_type.19.refs_0_, f32[272,1024]{1,0:T(8,128)} %convert_element_type.21.refs_1_, f32[272,1024]{1,0:T(8,128)} %convert_element_type.23.refs_2_), custom_call_target="tpu_custom_call" | custom-call | tf_op jit(solution)/shard_map/finish/pallas_call | solution.py:239
  (14 shorter events, 0.9 us)
Async XLA Ops:
  15.4 5.3 %copy-start.1 = (bf16[1,1024,256]{2,1,0:T(8,128)(2,1)S(1)}, bf16[1,1024,256]{2,1,0:T(8,128)(2,1)}, u32[]{:S(2)}) copy-start(bf16[1,1024,256]{2,1,0:T(8,128)(2,1)} %param.5) | copy-start | bytes 1572868
  15.4 54.4 %all-to-all-start = ((bf16[8,512,256]{2,1,0:T(8,128)(2,1)}), bf16[8,512,256]{2,1,0:T(8,128)(2,1)S(1)}, u32[]{:S(2)}, u32[]{:S(2)}) async-start(bf16[8,512,256]{2,1,0:T(8,128)(2,1)} %regroup.1), calls=%async_computation | async-start | bytes 4194304 | tf_op jit(solution)/shard_map/all_to_all | solution.py:264
  20.8 16.0 %collective-permute-start.2 = (bf16[1024,256]{1,0:T(8,128)(2,1)S(1)}, bf16[1024,256]{1,0:T(8,128)(2,1)S(1)}, u32[]{:S(2)}, u32[]{:S(2)}) collective-permute-start(bf16[1024,256]{1,0:T(8,128)(2,1)S(1)} %bitcast.11), channel_id=1, source_target_pairs={{0,3},{1,0},{2,1},{3,2},{4,7},{5,4},{6,5},{7,6},{8,11},{9,8},{10,9... | collective-permute-start | bytes 1572872 | tf_op jit(solution)/shard_map/ppermute | solution.py:257
  24.4 24.6 %collective-permute-start.1 = (bf16[1024,256]{1,0:T(8,128)(2,1)S(1)}, bf16[1024,256]{1,0:T(8,128)(2,1)S(1)}, u32[]{:S(2)}, u32[]{:S(2)}) collective-permute-start(bf16[1024,256]{1,0:T(8,128)(2,1)S(1)} %bitcast.12), channel_id=1, source_target_pairs={{0,1},{1,2},{2,3},{3,0},{4,5},{5,6},{6,7},{7,4},{8,9},{9,10},{10,1... | collective-permute-start | bytes 1572872 | tf_op jit(solution)/shard_map/ppermute | solution.py:257
  24.4 45.4 %collective-permute-start = (bf16[1024,256]{1,0:T(8,128)(2,1)S(1)}, bf16[1024,256]{1,0:T(8,128)(2,1)S(1)}, u32[]{:S(2)}, u32[]{:S(2)}) collective-permute-start(bf16[1024,256]{1,0:T(8,128)(2,1)S(1)} %bitcast.13), channel_id=1, source_target_pairs={{0,2},{1,3},{2,0},{3,1},{4,6},{5,7},{6,4},{7,5},{8,10},{9,11},{10,... | collective-permute-start | bytes 1572872 | tf_op jit(solution)/shard_map/ppermute | solution.py:257
  36.8 12.2 %copy-start.4 = (bf16[1024,256]{1,0:T(8,128)(2,1)}, bf16[1024,256]{1,0:T(8,128)(2,1)S(1)}, u32[]{:S(2)}) copy-start(bf16[1024,256]{1,0:T(8,128)(2,1)S(1)} %collective-permute-done.2.refs_3_.c_ref) | copy-start | bytes 1572868
  49.0 0.8 copy-start.3
  69.8 0.8 copy-start.2
  69.8 1.5 copy-start
  113.8 43.3 %collective-permute-start.5 = (f16[272,1024]{1,0:T(8,128)(2,1)S(1)}, f16[272,1024]{1,0:T(8,128)(2,1)S(1)}, u32[]{:S(2)}, u32[]{:S(2)}) collective-permute-start(f16[272,1024]{1,0:T(8,128)(2,1)S(1)} %convert_element_type.22), channel_id=1, source_target_pairs={{0,1},{1,2},{2,3},{3,0},{4,5},{5,6},{6,7},{7,4},{8,9},{9,10},{10,1... | collective-permute-start | bytes 1671176 | tf_op jit(solution)/shard_map/ppermute | solution.py:257
  127.4 30.8 %collective-permute-start.4 = (f16[272,1024]{1,0:T(8,128)(2,1)S(1)}, f16[272,1024]{1,0:T(8,128)(2,1)S(1)}, u32[]{:S(2)}, u32[]{:S(2)}) collective-permute-start(f16[272,1024]{1,0:T(8,128)(2,1)S(1)} %convert_element_type.20), channel_id=1, source_target_pairs={{0,3},{1,0},{2,1},{3,2},{4,7},{5,4},{6,5},{7,6},{8,11},{9,8},{10,9... | collective-permute-start | bytes 1671176 | tf_op jit(solution)/shard_map/ppermute | solution.py:257
  144.9 24.4 %collective-permute-start.3 = (f16[272,1024]{1,0:T(8,128)(2,1)S(1)}, f16[272,1024]{1,0:T(8,128)(2,1)S(1)}, u32[]{:S(2)}, u32[]{:S(2)}) collective-permute-start(f16[272,1024]{1,0:T(8,128)(2,1)S(1)} %convert_element_type.18), channel_id=1, source_target_pairs={{0,2},{1,3},{2,0},{3,1},{4,6},{5,7},{6,4},{7,5},{8,10},{9,11},{10,... | collective-permute-start | bytes 1671176 | tf_op jit(solution)/shard_map/ppermute | solution.py:257

commit v2 on v1

v2 whole, which is shorter than its diff:
```python
import functools
import math

import jax
import jax.numpy as jnp
from jax import lax
from jax.experimental import pallas as pl
from jax.experimental.pallas import tpu as pltpu
from jax.sharding import PartitionSpec as P


PRIOR_MASS = 1.0
SEND_SCALE = 512.0
MASS_SCALE = 8.0
PAD = 16
NT = (((1,), (1,)), ((), ()))


def regroup_kernel(ids_ref, x_ref, out_ref, dest_ref):
    lines, width = ids_ref.shape
    clusters, per, dim = out_ref.shape
    ids = ids_ref[...]
    upto = (
        lax.broadcasted_iota(jnp.int32, (width, width), 0)
        <= lax.broadcasted_iota(jnp.int32, (width, width), 1)
    )
    upto = jnp.where(upto, 1.0, 0.0).astype(jnp.bfloat16)
    before = (
        lax.broadcasted_iota(jnp.int32, (lines, lines), 1)
        < lax.broadcasted_iota(jnp.int32, (lines, lines), 0)
    )
    before = jnp.where(before, 1.0, 0.0).astype(jnp.bfloat16)
    ones = jnp.ones((width, width), jnp.bfloat16)
    dest = jnp.zeros((lines, width), jnp.float32)
    for c in range(clusters):
        mask = ids == c
        hot = jnp.where(mask, 1.0, 0.0).astype(jnp.bfloat16)
        within = jnp.dot(hot, upto, preferred_element_type=jnp.float32)
        total = jnp.dot(hot, ones, preferred_element_type=jnp.float32)
        ahead = jnp.dot(before, total.astype(jnp.bfloat16), preferred_element_type=jnp.float32)
        dest = jnp.where(mask, within + ahead + float(c * per - 1), dest)
    dest_ref[...] = dest.astype(jnp.int32)

    @pl.loop(0, clusters)
    def _(c):
        slot = lax.broadcasted_iota(jnp.int32, (per, 2 * width), 0) + c * per
        total = jnp.zeros((per, dim), jnp.float32)
        for j in range(0, lines, 2):
            row = jnp.concatenate([dest_ref[j : j + 1, :], dest_ref[j + 1 : j + 2, :]], axis=1)
            hot = jnp.where(row == slot, 1.0, 0.0).astype(jnp.bfloat16)
            total = total + jnp.dot(
                hot, x_ref[j * width : (j + 2) * width, :], preferred_element_type=jnp.float32
            )
        out_ref[c] = total.astype(out_ref.dtype)


def regroup(ids, x, clusters):
    rows, dim = x.shape
    width = 128
    lines = rows // width
    return pl.pallas_call(
        regroup_kernel,
        out_shape=jax.ShapeDtypeStruct((clusters, rows // clusters, dim), x.dtype),
        scratch_shapes=[pltpu.VMEM((lines, width), jnp.int32)],
        cost_estimate=pl.CostEstimate(
            flops=2 * rows * rows * dim, bytes_accessed=4 * rows * dim, transcendentals=0
        ),
        name="regroup",
    )(ids.reshape(lines, width), x)


def half_norms(c, factor):
    sq = c.astype(jnp.float32)
    sq = sq * sq
    high = sq.astype(jnp.bfloat16)
    low = (sq - high.astype(jnp.float32)).astype(jnp.bfloat16)
    ones = jnp.ones((8, c.shape[1]), jnp.bfloat16)
    total = lax.dot_general(ones, high, NT, preferred_element_type=jnp.float32)
    total = total + lax.dot_general(ones, low, NT, preferred_element_type=jnp.float32)
    return total[0:1] * (0.5 * factor)


def logits_of(x, c, h, factor):
    s = lax.dot_general(x, c, NT, preferred_element_type=jnp.float32)
    return s * factor - h


def stats_kernel(factor, lanes, tile, members, merge, last, x_ref, *refs):
    c_refs = refs[:members]
    old_ref = refs[members] if merge else None
    st_ref, h_ref, l_ref = refs[-3:]
    sub = c_refs[0].shape[0]
    for j in range(members):
        h_ref[:, j * sub : (j + 1) * sub] = half_norms(c_refs[j][...], factor)
    lane = lax.broadcasted_iota(jnp.int32, (tile, 128), 1)

    @pl.loop(0, x_ref.shape[0] // tile)
    def _(i):
        at_rows = pl.ds(pl.multiple_of(i * tile, tile), tile)
        x = x_ref[at_rows, :]
        top = None
        for j in range(members):
            for k in range(0, sub, lanes):
                at = j * sub + k
                l = logits_of(x, c_refs[j][k : k + lanes, :], h_ref[:, at : at + lanes], factor)
                l_ref[:, at : at + lanes] = l
                for q in range(0, lanes, 128):
                    part = l[:, q : q + 128]
                    top = part if top is None else jnp.maximum(top, part)
        top = jnp.broadcast_to(jnp.max(top, axis=1, keepdims=True), (tile, 128))
        if merge:
            old = old_ref[at_rows, :]
            old_top = jnp.broadcast_to(old[:, 0:1], (tile, 128))
            old_sum = jnp.broadcast_to(old[:, 1:2], (tile, 128))
            top = jnp.maximum(top, old_top)
        total = jnp.zeros((tile, 128), jnp.float32)
        for at in range(0, members * sub, 128):
            total = total + jnp.exp(l_ref[:, at : at + 128] - top)
        total = jnp.broadcast_to(jnp.sum(total, axis=1, keepdims=True), (tile, 128))
        if merge:
            total = total + old_sum * jnp.exp(old_top - top)
        if last:
            total = 1.0 / total
        st_ref[at_rows, :] = jnp.where(lane == 0, top, total)


def stats(x, shards, factor, tile, old, last):
    rows, dim = x.shape
    members, sub = len(shards), shards[0].shape[0]
    lanes = min(256, sub)
    merge = old is not None
    return pl.pallas_call(
        functools.partial(stats_kernel, factor, lanes, tile, members, merge, last),
        out_shape=jax.ShapeDtypeStruct((rows, 128), jnp.float32),
        scratch_shapes=[
            pltpu.VMEM((1, members * sub), jnp.float32),
            pltpu.VMEM((tile, members * sub), jnp.float32),
        ],
        cost_estimate=pl.CostEstimate(
            flops=2 * rows * members * sub * dim,
            bytes_accessed=2 * dim * (rows + members * sub) + 1024 * rows,
            transcendentals=rows * members * sub,
        ),
        name="stats",
    )(x, *shards, *([old] if merge else []))


def weigh_kernel(factor, lanes, tile, send, x_ref, st_ref, c_ref, *refs):
    if send:
        out_ref, h_ref, xt_ref, acc_ref = refs
    else:
        acc_ref, h_ref, xt_ref = refs
    dim = x_ref.shape[1]
    sub = c_ref.shape[0]
    h_ref[...] = half_norms(c_ref[...], factor)
    xt_ref[dim:, :] = jnp.ones((PAD, tile), jnp.bfloat16)
    acc_ref[...] = jnp.zeros_like(acc_ref)

    @pl.loop(0, x_ref.shape[0] // tile)
    def _(i):
        at_rows = pl.ds(pl.multiple_of(i * tile, tile), tile)
        x = x_ref[at_rows, :]
        xt_ref[:dim, :] = x.T
        xt = xt_ref[...]
        m = jnp.broadcast_to(st_ref[at_rows, 0:1], (tile, lanes))
        inv = jnp.broadcast_to(st_ref[at_rows, 1:2], (tile, lanes))
        for k in range(0, sub, lanes):
            l = logits_of(x, c_ref[k : k + lanes, :], h_ref[:, k : k + lanes], factor)
            r = (jnp.exp(l - m) * inv).astype(jnp.bfloat16)
            acc_ref[:, k : k + lanes] += jnp.dot(xt, r, preferred_element_type=jnp.float32)

    if send:
        mass = acc_ref[dim : dim + 1, :]
        scale = SEND_SCALE / jnp.maximum(mass, 1e-30)
        out_ref[:dim, :] = acc_ref[:dim, :] * scale
        mass = mass * MASS_SCALE
        parts = []
        for _ in range(3):
            part = mass.astype(jnp.bfloat16).astype(jnp.float32)
            parts.append(part)
            mass = mass - part
        rest = jnp.zeros((PAD - 3, sub), jnp.float32)
        out_ref[dim:, :] = jnp.concatenate(parts + [rest], axis=0)


def weigh(x, st, c, factor, tile, send):
    rows, dim = x.shape
    sub = c.shape[0]
    lanes = min(256, sub)
    acc = (dim + PAD, sub)
    scratch = [pltpu.VMEM((1, sub), jnp.float32), pltpu.VMEM((dim + PAD, tile), jnp.bfloat16)]
    if send:
        scratch.append(pltpu.VMEM(acc, jnp.float32))
    return pl.pallas_call(
        functools.partial(weigh_kernel, factor, lanes, tile, send),
        out_shape=jax.ShapeDtypeStruct(acc, jnp.float32),
        scratch_shapes=scratch,
        cost_estimate=pl.CostEstimate(
            flops=4 * rows * sub * dim,
            bytes_accessed=2 * dim * (rows + sub) + 1024 * rows,
            transcendentals=rows * sub,
        ),
        name="weigh",
    )(x, st, c)


def finish_kernel(own_ref, c_ref, *refs):
    arrived, out_ref, mass_ref = refs[:-2], refs[-2], refs[-1]
    dim = c_ref.shape[1]
    total = own_ref[:dim, :]
    mass = own_ref[dim : dim + 1, :]
    for ref in arrived:
        parts = ref[dim:, :]
        part = (parts[0:1] + parts[1:2] + parts[2:3]) * (1.0 / MASS_SCALE)
        total = total + ref[:dim, :] * (part * (1.0 / SEND_SCALE))
        mass = mass + part
    mass_ref[...] = mass
    prior = PRIOR_MASS * c_ref[...].astype(jnp.float32)
    inv = 1.0 / (mass + PRIOR_MASS)
    out_ref[...] = (total * inv).T + prior * jnp.broadcast_to(inv, (8, inv.shape[1])).T[:, 0:1]


def finish(own, c, arrived):
    sub, dim = c.shape
    return pl.pallas_call(
        finish_kernel,
        out_shape=[
            jax.ShapeDtypeStruct((sub, dim), jnp.float32),
            jax.ShapeDtypeStruct((1, sub), jnp.float32),
        ],
        name="finish",
    )(own, c, *arrived)


def local(embeddings, cluster_ids, centroids):
    rows, dim = embeddings.shape
    clusters = lax.axis_size("group")
    members = lax.axis_size("member")
    factor = 2.0 / math.sqrt(dim)
    own = centroids[0]

    def rotate(value, step):
        return lax.ppermute(
            value, "member", [(i, (i + step) % members) for i in range(members)]
        )

    tile = min(512, rows)
    order = sorted(range(1, members), key=lambda d: abs(d - members / 2))
    arrived = {}
    for d in order:
        arrived[d] = rotate(own, d)
    packed = regroup(cluster_ids, embeddings, clusters)
    x = lax.all_to_all(packed, "group", split_axis=0, concat_axis=0, tiled=True)
    x = x.reshape(rows, dim)
    st = stats(x, [own] + [arrived[d] for d in order[:-1]], factor, tile, None, members == 1)
    for d in order[-1:]:
        st = stats(x, [arrived[d]], factor, tile, st, True)
    back = []
    for d in order:
        partial = weigh(x, st, arrived[d], factor, tile, True).astype(jnp.float16)
        back.append(rotate(partial, -d).astype(jnp.float32))
    mine = weigh(x, st, own, factor, tile, False)
    updated, mass = finish(mine, own, back)
    return updated[None], mass


def solution(mesh):
    placed = (P(("group", "member"), None), P(("group", "member")), P("group", "member", None))
    return jax.shard_map(
        local,
        mesh=mesh,
        in_specs=placed,
        out_specs=(P("group", "member", None), P("group", "member")),
        check_vma=False,
    )
```

time: 175 us -> 181 us (1.034)
  waiting for transfers between devices: 53.6 us -> 42.4 us
  starting transfers between devices: 14 us -> 24.6 us
  Pallas kernels: 95.3 us -> 103 us
    ppermute x6, waiting for transfers between devices: 53.6 us -> 42.4 us  [rotate(): lax.ppermute(value, 'member', [(i, (i + step) % members) for i in range(m...]
    ppermute x6, starting transfers between devices: 8.64 us -> 19.2 us  [rotate(): lax.ppermute(value, 'member', [(i, (i + step) % members) for i in range(m...]
    pallas_call x6 -> x7, Pallas kernels: 91.2 us -> 99.4 us  [the longest x4 52.2 us: weigh(): pl.pallas_call(functools.partial(weigh_kernel, factor, lanes, tile, send)...]
  transfers between devices with their start and end apart: 7 -> 7, of which waited for: 4 -> 3; matrix products, arithmetic and copies ran while one was open for 3% -> 3% of each run, Pallas kernels for 21% -> 34%
where the time goes in v2:
time: 181 us
  Pallas kernels  103 us (57%)
  waiting for transfers between devices  42.4 us (23%)
  starting transfers between devices  24.6 us (14%)
  other arithmetic  7.25 us (4%)
  local copies, waits for them, and re-layouts  2.3 us (1%)
    pallas_call x4, Pallas kernels, weigh(): pl.pallas_call(functools.partial(weigh_kernel, factor, lanes, tile, send)...  52.2 us
    ppermute x6, waiting for transfers between devices, rotate(): lax.ppermute(value, 'member', [(i, (i + step) % members) for i in range(m...  42.4 us
    pallas_call x2, Pallas kernels, stats(): pl.pallas_call(functools.partial(stats_kernel, factor, lanes, tile, membe...  33.4 us
    ppermute x6, starting transfers between devices, rotate(): lax.ppermute(value, 'member', [(i, (i + step) % members) for i in range(m...  19.2 us
    pallas_call x1, Pallas kernels, regroup(): pl.pallas_call(regroup_kernel, out_shape=jax.ShapeDtypeStruct((clusters,...  13.8 us
    all_to_all x1, starting transfers between devices, local(): x = lax.all_to_all(packed, 'group', split_axis=0, concat_axis=0, tiled=True)  5.33 us
    pallas_call x1, Pallas kernels, finish(): pl.pallas_call(finish_kernel, out_shape=[jax.ShapeDtypeStruct((sub, dim),...  4.08 us
    convert_element_type x3, other arithmetic, local(): partial = weigh(x, st, arrived[d], factor, tile, True).astype(jnp.float16)  3.98 us
  transfers between devices with their start and end apart: 7, of which 3 were waited for; matrix products, arithmetic and copies ran while one was open for 3% of the time, Pallas kernels for 34%

profile of v2, /device:TPU:0, one launch (start us, length us, event | category | flops | bytes accessed | tf_op | source)
XLA Modules:
  0.0 180.7 jit_solution(5526844457900478698)
XLA Ops:
  0.6 13.8 %regroup.1 = bf16[8,512,256]{2,1,0:T(8,128)(2,1)} custom-call(s32[32,128]{1,0:T(8,128)} %bitcast.17, bf16[4096,256]{1,0:T(8,128)(2,1)} %x_ref.1), custom_call_target="tpu_custom_call" | custom-call | flops 8589934592 | bytes 4194304 | tf_op jit(solution)/shard_map/regroup/pallas_call | solution.py:61
  14.5 5.3 %all-to-all-start = ((bf16[8,512,256]{2,1,0:T(8,128)(2,1)}), bf16[8,512,256]{2,1,0:T(8,128)(2,1)S(1)}, u32[]{:S(2)}, u32[]{:S(2)}) async-start(bf16[8,512,256]{2,1,0:T(8,128)(2,1)} %regroup.1), calls=%async_computation | async-start | bytes 4194304 | tf_op jit(solution)/shard_map/all_to_all | solution.py:253
  19.8 1.6 collective-permute-start.2
  21.4 2.6 %collective-permute-start.1 = (bf16[1024,256]{1,0:T(8,128)(2,1)S(1)}, bf16[1024,256]{1,0:T(8,128)(2,1)S(1)}, u32[]{:S(2)}, u32[]{:S(2)}) collective-permute-start(bf16[1024,256]{1,0:T(8,128)(2,1)S(1)} %bitcast.14), channel_id=1, source_target_pairs={{0,2},{1,3},{2,0},{3,1},{4,6},{5,7},{6,4},{7,5},{8,10},{9,11},{10,... | collective-permute-start | bytes 1572872 | tf_op jit(solution)/shard_map/ppermute | solution.py:243
  24.0 1.3 collective-permute-start
  25.4 11.2 %collective-permute-done.2.refs_2_.c_ref = bf16[1024,256]{1,0:T(8,128)(2,1)S(1)} collective-permute-done((bf16[1024,256]{1,0:T(8,128)(2,1)S(1)}, bf16[1024,256]{1,0:T(8,128)(2,1)S(1)}, u32[]{:S(2)}, u32[]{:S(2)}) %collective-permute-start.2) | collective-permute-done | bytes 524320 | tf_op jit(solution)/shard_map/ppermute | solution.py:243
  36.6 0.8 copy-done.3
  37.4 21.2 %collective-permute-done.1.refs_1_.c_ref = bf16[1024,256]{1,0:T(8,128)(2,1)S(1)} collective-permute-done((bf16[1024,256]{1,0:T(8,128)(2,1)S(1)}, bf16[1024,256]{1,0:T(8,128)(2,1)S(1)}, u32[]{:S(2)}, u32[]{:S(2)}) %collective-permute-start.1) | collective-permute-done | bytes 524320 | tf_op jit(solution)/shard_map/ppermute | solution.py:243
  60.1 22.0 %stats.2.refs_1_ = f32[4096,128]{1,0:T(8,128)} custom-call(bf16[4096,256]{1,0:T(8,128)(2,1)} %bitcast.4, bf16[1024,256]{1,0:T(8,128)(2,1)} %bitcast.10, bf16[1024,256]{1,0:T(8,128)(2,1)} %copy-done.2, bf16[1024,256]{1,0:T(8,128)(2,1)} %copy-done.3), custom_call_target="tpu_custom_call" | custom-call | flops 6442450944 | bytes 7864320 | tf_op jit(solution)/shard_map/stats/pallas_call | solution.py:132
  82.0 11.4 %stats.3.st_ref = f32[4096,128]{1,0:T(8,128)} custom-call(bf16[4096,256]{1,0:T(8,128)(2,1)} %bitcast.5, bf16[1024,256]{1,0:T(8,128)(2,1)} %collective-permute-done.refs_0_.c_ref, f32[4096,128]{1,0:T(8,128)} %stats.2.refs_1_), custom_call_target="tpu_custom_call" | custom-call | flops 2147483648 | bytes 6815744 | tf_op jit(solution)/shard_map/stats/pallas_call | solution.py:132
  93.4 13.1 %weigh.7 = f32[272,1024]{1,0:T(8,128)} custom-call(bf16[4096,256]{1,0:T(8,128)(2,1)} %bitcast.6, f32[4096,128]{1,0:T(8,128)} %stats.3.st_ref, bf16[1024,256]{1,0:T(8,128)(2,1)} %collective-permute-done.refs_0_.c_ref), custom_call_target="tpu_custom_call" | custom-call | flops 4294967296 | bytes 6815744 | tf_op jit(solution)/shard_map/weigh/pallas_call | solution.py:194
  106.5 1.3 convert_element_type.22
  107.8 10.0 %collective-permute-start.5 = (f16[272,1024]{1,0:T(8,128)(2,1)S(1)}, f16[272,1024]{1,0:T(8,128)(2,1)S(1)}, u32[]{:S(2)}, u32[]{:S(2)}) collective-permute-start(f16[272,1024]{1,0:T(8,128)(2,1)S(1)} %convert_element_type.22), channel_id=1, source_target_pairs={{0,1},{1,2},{2,3},{3,0},{4,5},{5,6},{6,7},{7,4},{8,9},{9,10},{10,1... | collective-permute-start | bytes 1671176 | tf_op jit(solution)/shard_map/ppermute | solution.py:243
  117.8 13.1 %weigh.6 = f32[272,1024]{1,0:T(8,128)} custom-call(bf16[4096,256]{1,0:T(8,128)(2,1)} %bitcast.7, f32[4096,128]{1,0:T(8,128)} %stats.3.st_ref, bf16[1024,256]{1,0:T(8,128)(2,1)} %copy-done.3), custom_call_target="tpu_custom_call" | custom-call | flops 4294967296 | bytes 6815744 | tf_op jit(solution)/shard_map/weigh/pallas_call | solution.py:194
  130.9 1.3 convert_element_type.20
  132.2 3.1 %collective-permute-start.4 = (f16[272,1024]{1,0:T(8,128)(2,1)S(1)}, f16[272,1024]{1,0:T(8,128)(2,1)S(1)}, u32[]{:S(2)}, u32[]{:S(2)}) collective-permute-start(f16[272,1024]{1,0:T(8,128)(2,1)S(1)} %convert_element_type.20), channel_id=1, source_target_pairs={{0,3},{1,0},{2,1},{3,2},{4,7},{5,4},{6,5},{7,6},{8,11},{9,8},{10,9... | collective-permute-start | bytes 1671176 | tf_op jit(solution)/shard_map/ppermute | solution.py:243
  135.3 13.1 %weigh.5 = f32[272,1024]{1,0:T(8,128)} custom-call(bf16[4096,256]{1,0:T(8,128)(2,1)} %bitcast.8, f32[4096,128]{1,0:T(8,128)} %stats.3.st_ref, bf16[1024,256]{1,0:T(8,128)(2,1)} %copy-done.2), custom_call_target="tpu_custom_call" | custom-call | flops 4294967296 | bytes 6815744 | tf_op jit(solution)/shard_map/weigh/pallas_call | solution.py:194
  148.3 1.3 convert_element_type.18
  150.3 13.0 %weigh.4.own_ref = f32[272,1024]{1,0:T(8,128)} custom-call(bf16[4096,256]{1,0:T(8,128)(2,1)} %bitcast.9, f32[4096,128]{1,0:T(8,128)} %stats.3.st_ref, bf16[1024,256]{1,0:T(8,128)(2,1)} %bitcast.11), custom_call_target="tpu_custom_call" | custom-call | flops 4294967296 | bytes 6815744 | tf_op jit(solution)/shard_map/weigh/pallas_call | solution.py:194
  163.3 1.1 convert_element_type.23.refs_2_
  164.4 1.1 convert_element_type.21.refs_1_
  165.5 10.0 %collective-permute-done.3 = f16[272,1024]{1,0:T(8,128)(2,1)S(1)} collective-permute-done((f16[272,1024]{1,0:T(8,128)(2,1)S(1)}, f16[272,1024]{1,0:T(8,128)(2,1)S(1)}, u32[]{:S(2)}, u32[]{:S(2)}) %collective-permute-start.3) | collective-permute-done | bytes 557088 | tf_op jit(solution)/shard_map/ppermute | solution.py:243
  175.5 1.1 convert_element_type.19.refs_0_
  176.6 4.1 %finish.1 = (f32[1024,256]{1,0:T(8,128)}, f32[1,1024]{1,0:T(1,128)}) custom-call(f32[272,1024]{1,0:T(8,128)} %weigh.4.own_ref, bf16[1024,256]{1,0:T(8,128)(2,1)} %bitcast.12, f32[272,1024]{1,0:T(8,128)} %convert_element_type.19.refs_0_, f32[272,1024]{1,0:T(8,128)} %convert_element_type.21.refs_1_, f32[272,1024]{1,0:T(8,128)} %convert_element_type.23.refs_2_), custom_call_target="tpu_custom_call" | custom-call | tf_op jit(solution)/shard_map/finish/pallas_call | solution.py:225
  (12 shorter events, 2.1 us)
Async XLA Ops:
  14.5 5.3 %copy-start.1 = (bf16[1,1024,256]{2,1,0:T(8,128)(2,1)S(1)}, bf16[1,1024,256]{2,1,0:T(8,128)(2,1)}, u32[]{:S(2)}) copy-start(bf16[1,1024,256]{2,1,0:T(8,128)(2,1)} %param.5) | copy-start | bytes 1572868
  14.5 44.1 %all-to-all-start = ((bf16[8,512,256]{2,1,0:T(8,128)(2,1)}), bf16[8,512,256]{2,1,0:T(8,128)(2,1)S(1)}, u32[]{:S(2)}, u32[]{:S(2)}) async-start(bf16[8,512,256]{2,1,0:T(8,128)(2,1)} %regroup.1), calls=%async_computation | async-start | bytes 4194304 | tf_op jit(solution)/shard_map/all_to_all | solution.py:253
  19.8 16.8 %collective-permute-start.2 = (bf16[1024,256]{1,0:T(8,128)(2,1)S(1)}, bf16[1024,256]{1,0:T(8,128)(2,1)S(1)}, u32[]{:S(2)}, u32[]{:S(2)}) collective-permute-start(bf16[1024,256]{1,0:T(8,128)(2,1)S(1)} %bitcast.13), channel_id=1, source_target_pairs={{0,1},{1,2},{2,3},{3,0},{4,5},{5,6},{6,7},{7,4},{8,9},{9,10},{10,1... | collective-permute-start | bytes 1572872 | tf_op jit(solution)/shard_map/ppermute | solution.py:243
  21.4 37.1 %collective-permute-start.1 = (bf16[1024,256]{1,0:T(8,128)(2,1)S(1)}, bf16[1024,256]{1,0:T(8,128)(2,1)S(1)}, u32[]{:S(2)}, u32[]{:S(2)}) collective-permute-start(bf16[1024,256]{1,0:T(8,128)(2,1)S(1)} %bitcast.14), channel_id=1, source_target_pairs={{0,2},{1,3},{2,0},{3,1},{4,6},{5,7},{6,4},{7,5},{8,10},{9,11},{10,... | collective-permute-start | bytes 1572872 | tf_op jit(solution)/shard_map/ppermute | solution.py:243
  24.0 58.0 %collective-permute-start = (bf16[1024,256]{1,0:T(8,128)(2,1)S(1)}, bf16[1024,256]{1,0:T(8,128)(2,1)}, u32[]{:S(2)}, u32[]{:S(2)}) collective-permute-start(bf16[1024,256]{1,0:T(8,128)(2,1)S(1)} %bitcast.15), channel_id=1, source_target_pairs={{0,3},{1,0},{2,1},{3,2},{4,7},{5,4},{6,5},{7,6},{8,11},{9,8},{10,9... | collective-permute-start | bytes 1572872 | tf_op jit(solution)/shard_map/ppermute | solution.py:243
  36.6 0.8 copy-start.3
  58.6 0.8 copy-start.2
  58.6 1.5 copy-start
  107.8 55.5 %collective-permute-start.5 = (f16[272,1024]{1,0:T(8,128)(2,1)S(1)}, f16[272,1024]{1,0:T(8,128)(2,1)S(1)}, u32[]{:S(2)}, u32[]{:S(2)}) collective-permute-start(f16[272,1024]{1,0:T(8,128)(2,1)S(1)} %convert_element_type.22), channel_id=1, source_target_pairs={{0,1},{1,2},{2,3},{3,0},{4,5},{5,6},{6,7},{7,4},{8,9},{9,10},{10,1... | collective-permute-start | bytes 1671176 | tf_op jit(solution)/shard_map/ppermute | solution.py:243
  132.2 32.2 %collective-permute-start.4 = (f16[272,1024]{1,0:T(8,128)(2,1)S(1)}, f16[272,1024]{1,0:T(8,128)(2,1)S(1)}, u32[]{:S(2)}, u32[]{:S(2)}) collective-permute-start(f16[272,1024]{1,0:T(8,128)(2,1)S(1)} %convert_element_type.20), channel_id=1, source_target_pairs={{0,3},{1,0},{2,1},{3,2},{4,7},{5,4},{6,5},{7,6},{8,11},{9,8},{10,9... | collective-permute-start | bytes 1671176 | tf_op jit(solution)/shard_map/ppermute | solution.py:243
  149.7 25.8 %collective-permute-start.3 = (f16[272,1024]{1,0:T(8,128)(2,1)S(1)}, f16[272,1024]{1,0:T(8,128)(2,1)S(1)}, u32[]{:S(2)}, u32[]{:S(2)}) collective-permute-start(f16[272,1024]{1,0:T(8,128)(2,1)S(1)} %convert_element_type.18), channel_id=1, source_target_pairs={{0,2},{1,3},{2,0},{3,1},{4,6},{5,7},{6,4},{7,5},{8,10},{9,11},{10,... | collective-permute-start | bytes 1671176 | tf_op jit(solution)/shard_map/ppermute | solution.py:243

commit v3 on v2

v3 whole, which is shorter than its diff:
```python
import functools
import math

import jax
import jax.numpy as jnp
from jax import lax
from jax.experimental import pallas as pl
from jax.experimental.pallas import tpu as pltpu
from jax.sharding import PartitionSpec as P


PRIOR_MASS = 1.0
SEND_SCALE = 512.0
MASS_SCALE = 8.0
PAD = 16
VMEM = 24 << 20
NT = (((1,), (1,)), ((), ()))


def regroup_kernel(ids_ref, x_ref, out_ref, dest_ref):
    lines, width = ids_ref.shape
    clusters, per, dim = out_ref.shape
    ids = ids_ref[...]
    upto = (
        lax.broadcasted_iota(jnp.int32, (width, width), 0)
        <= lax.broadcasted_iota(jnp.int32, (width, width), 1)
    )
    upto = jnp.where(upto, 1.0, 0.0).astype(jnp.bfloat16)
    before = (
        lax.broadcasted_iota(jnp.int32, (lines, lines), 1)
        < lax.broadcasted_iota(jnp.int32, (lines, lines), 0)
    )
    before = jnp.where(before, 1.0, 0.0).astype(jnp.bfloat16)
    ones = jnp.ones((width, width), jnp.bfloat16)
    dest = jnp.zeros((lines, width), jnp.float32)
    for c in range(clusters):
        mask = ids == c
        hot = jnp.where(mask, 1.0, 0.0).astype(jnp.bfloat16)
        within = jnp.dot(hot, upto, preferred_element_type=jnp.float32)
        total = jnp.dot(hot, ones, preferred_element_type=jnp.float32)
        ahead = jnp.dot(before, total.astype(jnp.bfloat16), preferred_element_type=jnp.float32)
        dest = jnp.where(mask, within + ahead + float(c * per - 1), dest)
    dest_ref[...] = dest.astype(jnp.int32)

    @pl.loop(0, clusters)
    def _(c):
        slot = lax.broadcasted_iota(jnp.int32, (per, 2 * width), 0) + c * per
        total = jnp.zeros((per, dim), jnp.float32)
        for j in range(0, lines, 2):
            row = jnp.concatenate([dest_ref[j : j + 1, :], dest_ref[j + 1 : j + 2, :]], axis=1)
            hot = jnp.where(row == slot, 1.0, 0.0).astype(jnp.bfloat16)
            total = total + jnp.dot(
                hot, x_ref[j * width : (j + 2) * width, :], preferred_element_type=jnp.float32
            )
        out_ref[c] = total.astype(out_ref.dtype)


def regroup(ids, x, clusters):
    rows, dim = x.shape
    width = 128
    lines = rows // width
    return pl.pallas_call(
        regroup_kernel,
        out_shape=jax.ShapeDtypeStruct((clusters, rows // clusters, dim), x.dtype),
        scratch_shapes=[pltpu.VMEM((lines, width), jnp.int32)],
        compiler_params=pltpu.CompilerParams(vmem_limit_bytes=VMEM),
        cost_estimate=pl.CostEstimate(
            flops=2 * rows * rows * dim, bytes_accessed=4 * rows * dim, transcendentals=0
        ),
        name="regroup",
    )(ids.reshape(lines, width), x)


def squares(v):
    sq = v.astype(jnp.float32)
    sq = sq * sq
    high = sq.astype(jnp.bfloat16)
    return high, (sq - high.astype(jnp.float32)).astype(jnp.bfloat16)


def half_norms(c, factor):
    ones = jnp.ones((c.shape[1], 128), jnp.bfloat16)
    high, low = squares(c)
    total = jnp.dot(high, ones, preferred_element_type=jnp.float32)
    total = total + jnp.dot(low, ones, preferred_element_type=jnp.float32)
    return total * (0.5 * factor)


def row_bounds(x, factor):
    ones = jnp.ones((8, x.shape[1]), jnp.bfloat16)
    high, low = squares(x)
    total = lax.dot_general(ones, high, NT, preferred_element_type=jnp.float32)
    total = total + lax.dot_general(ones, low, NT, preferred_element_type=jnp.float32)
    return total[0:1] * (0.5 * factor)


def logits_of(c, x, h, factor):
    s = lax.dot_general(c, x, NT, preferred_element_type=jnp.float32)
    return s * factor - jnp.concatenate([h] * (x.shape[0] // 128), axis=1)


def fold(value, op):
    rows, cols = value.shape
    return op(value.reshape(rows // 8, 8, cols), axis=0)


def stats_kernel(factor, step, tile, members, merge, rest, x_ref, *refs):
    c_refs, refs = refs[:members], refs[members:]
    old_ref, refs = (refs[0], refs[1:]) if merge else (None, refs)
    rest_refs, refs = refs[:rest], refs[rest:]
    st_ref, h_ref = refs[:2]
    sub = c_refs[0].shape[0]
    rows = x_ref.shape[0]
    last = len(refs) > 2
    for j in range(members):
        h_ref[j * sub : (j + 1) * sub, :] = half_norms(c_refs[j][...], factor)

    @pl.loop(0, rows // tile)
    def _(i):
        at = pl.ds(pl.multiple_of(i * tile, tile), tile)
        x = x_ref[at, :]
        if merge:
            bound = old_ref[0:1, at]
            total = old_ref[1:2, at]
        else:
            bound = row_bounds(x, factor)
            total = jnp.zeros((1, tile), jnp.float32)
        wide = jnp.zeros((8, tile), jnp.float32)
        for j in range(members):
            for k in range(0, sub, step):
                h = h_ref[j * sub + k : j * sub + k + step, :]
                l = logits_of(c_refs[j][k : k + step, :], x, h, factor)
                wide = wide + fold(jnp.exp(l - bound), jnp.sum)
        st_ref[0:1, at] = bound
        st_ref[1:2, at] = total + jnp.sum(wide, axis=0, keepdims=True)

    if not last:
        return
    buf_ref, l_ref = refs[2:]

    @pl.when(jnp.min(st_ref[1:2, :]) < 1e-24)
    def _():
        st_ref[0:1, :] = jnp.full((1, rows), -3e38, jnp.float32)
        st_ref[1:2, :] = jnp.zeros((1, rows), jnp.float32)
        for ref in tuple(c_refs) + tuple(rest_refs):
            pltpu.sync_copy(ref, buf_ref)
            h_ref[0:sub, :] = half_norms(buf_ref[...], factor)

            @pl.loop(0, rows // 128)
            def _(i):
                at = pl.ds(pl.multiple_of(i * 128, 128), 128)
                l_ref[...] = logits_of(buf_ref[...], x_ref[at, :], h_ref[0:sub, :], factor)
                was = st_ref[0:1, at]
                top = jnp.max(fold(l_ref[...], jnp.max), axis=0, keepdims=True)
                top = jnp.maximum(top, was)
                total = fold(jnp.exp(l_ref[...] - top), jnp.sum)
                total = jnp.sum(total, axis=0, keepdims=True)
                st_ref[0:1, at] = top
                st_ref[1:2, at] = total + st_ref[1:2, at] * jnp.exp(was - top)

    st_ref[1:2, :] = 1.0 / st_ref[1:2, :]


def stats(x, shards, factor, tile, old=None, rest=None):
    rows, dim = x.shape
    members, sub = len(shards), shards[0].shape[0]
    step = min(256, sub)
    merge, last = old is not None, rest is not None
    rest = rest or []
    whole = pl.BlockSpec(memory_space=pltpu.VMEM)
    scratch = [pltpu.VMEM((members * sub, 128), jnp.float32)]
    if last:
        scratch += [pltpu.VMEM((sub, dim), jnp.bfloat16), pltpu.VMEM((sub, 128), jnp.float32)]
    return pl.pallas_call(
        functools.partial(stats_kernel, factor, step, tile, members, merge, len(rest)),
        in_specs=[whole] * (1 + members + merge) + [pl.BlockSpec(memory_space=pl.ANY)] * len(rest),
        out_specs=whole,
        out_shape=jax.ShapeDtypeStruct((8, rows), jnp.float32),
        scratch_shapes=scratch,
        compiler_params=pltpu.CompilerParams(vmem_limit_bytes=VMEM),
        cost_estimate=pl.CostEstimate(
            flops=2 * rows * members * sub * dim,
            bytes_accessed=2 * dim * (rows + members * sub),
            transcendentals=rows * members * sub,
        ),
        name="stats",
    )(x, *shards, *([old] if merge else []), *rest)


def weigh_kernel(factor, step, tile, send, x_ref, st_ref, c_ref, *refs):
    if send:
        out_ref, h_ref, acc_ref, mass_ref = refs
    else:
        acc_ref, mass_ref, h_ref = refs
    dim = x_ref.shape[1]
    sub = c_ref.shape[0]
    h_ref[...] = half_norms(c_ref[...], factor)
    acc_ref[...] = jnp.zeros_like(acc_ref)
    mass_ref[...] = jnp.zeros_like(mass_ref)

    @pl.loop(0, x_ref.shape[0] // tile)
    def _(i):
        at = pl.ds(pl.multiple_of(i * tile, tile), tile)
        x = x_ref[at, :]
        top = st_ref[0:1, at]
        inv = st_ref[1:2, at]
        for k in range(0, sub, step):
            ks = slice(k, k + step)
            l = logits_of(c_ref[ks, :], x, h_ref[ks, :], factor)
            r = (jnp.exp(l - top) * inv).astype(jnp.bfloat16)
            acc_ref[ks, :] += jnp.dot(r, x, preferred_element_type=jnp.float32)
            r = r.astype(jnp.float32)
            part = r[:, 0:128]
            for q in range(128, tile, 128):
                part = part + r[:, q : q + 128]
            mass_ref[ks, :] += part

    mass = jnp.broadcast_to(jnp.sum(mass_ref[...], axis=1, keepdims=True), (sub, 128))
    if not send:
        mass_ref[...] = mass
        return
    scale = jnp.concatenate([SEND_SCALE / jnp.maximum(mass, 1e-30)] * (dim // 128), axis=1)
    out_ref[0:sub, :] = acc_ref[...] * scale
    mass = mass.T[0:1, :] * MASS_SCALE
    parts = []
    for _ in range(3):
        part = mass.astype(jnp.bfloat16).astype(jnp.float32)
        parts += [part[:, k : k + dim] for k in range(0, sub, dim)]
        mass = mass - part
    rest = out_ref.shape[0] - sub - len(parts)
    parts.append(jnp.zeros((rest, dim), jnp.float32))
    out_ref[sub:, :] = jnp.concatenate(parts, axis=0)


def weigh(x, st, c, factor, tile, send):
    rows, dim = x.shape
    sub = c.shape[0]
    step = min(256, sub)
    sums, masses = (sub, dim), (sub, 128)
    scratch = [pltpu.VMEM((sub, 128), jnp.float32)]
    if send:
        scratch += [pltpu.VMEM(sums, jnp.float32), pltpu.VMEM(masses, jnp.float32)]
        out = jax.ShapeDtypeStruct((sub + PAD, dim), jnp.float32)
    else:
        out = [jax.ShapeDtypeStruct(sums, jnp.float32), jax.ShapeDtypeStruct(masses, jnp.float32)]
    return pl.pallas_call(
        functools.partial(weigh_kernel, factor, step, tile, send),
        out_shape=out,
        scratch_shapes=scratch,
        compiler_params=pltpu.CompilerParams(vmem_limit_bytes=VMEM),
        cost_estimate=pl.CostEstimate(
            flops=4 * rows * sub * dim,
            bytes_accessed=2 * dim * (rows + sub),
            transcendentals=rows * sub,
        ),
        name="weigh",
    )(x, st, c)


def finish_kernel(own_ref, own_mass_ref, c_ref, *refs):
    arrived, out_ref, mass_ref = refs[:-2], refs[-2], refs[-1]
    sub, dim = c_ref.shape

    def wide(value):
        return jnp.concatenate([value] * (dim // 128), axis=1)

    total = own_ref[...]
    mass = own_mass_ref[...]
    for ref in arrived:
        count = sub // dim
        part = None
        for p in range(3):
            row = [ref[sub + p * count + q : sub + p * count + q + 1, :] for q in range(count)]
            row = jnp.concatenate(row, axis=1)
            part = row if part is None else part + row
        part = jnp.broadcast_to(part * (1.0 / MASS_SCALE), (128, sub)).T
        total = total + ref[0:sub, :] * wide(part * (1.0 / SEND_SCALE))
        mass = mass + part
    mass_ref[...] = mass.T[0:1, :]
    prior = PRIOR_MASS * c_ref[...].astype(jnp.float32)
    out_ref[...] = (total + prior) * wide(1.0 / (mass + PRIOR_MASS))


def finish(own, own_mass, c, arrived):
    sub, dim = c.shape
    return pl.pallas_call(
        finish_kernel,
        out_shape=[
            jax.ShapeDtypeStruct((sub, dim), jnp.float32),
            jax.ShapeDtypeStruct((1, sub), jnp.float32),
        ],
        compiler_params=pltpu.CompilerParams(vmem_limit_bytes=VMEM),
        name="finish",
    )(own, own_mass, c, *arrived)


def send_order(members):
    return sorted(range(1, members), key=lambda d: abs(d - members / 2))


def local(embeddings, cluster_ids, centroids):
    rows, dim = embeddings.shape
    clusters = lax.axis_size("group")
    members = lax.axis_size("member")
    factor = 2.0 / math.sqrt(dim)
    own = centroids[0]

    def rotate(value, step):
        return lax.ppermute(
            value, "member", [(i, (i + step) % members) for i in range(members)]
        )

    tile = min(1024, rows)
    order = send_order(members)
    arrived = {}
    for d in order:
        arrived[d] = rotate(own, d)
    packed = regroup(cluster_ids, embeddings, clusters)
    x = lax.all_to_all(packed, "group", split_axis=0, concat_axis=0, tiled=True)
    x = x.reshape(rows, dim)
    if members == 1:
        st = stats(x, [own], factor, tile, None, [])
    else:
        early = [own] + [arrived[d] for d in order[:-1]]
        st = stats(x, early, factor, tile)
        st = stats(x, [arrived[order[-1]]], factor, tile, st, early)
    back = []
    for d in order:
        partial = weigh(x, st, arrived[d], factor, tile, True).astype(jnp.float16)
        back.append(rotate(partial, -d).astype(jnp.float32))
    mine, mine_mass = weigh(x, st, own, factor, tile, False)
    updated, mass = finish(mine, mine_mass, own, back)
    return updated[None], mass


def solution(mesh):
    placed = (P(("group", "member"), None), P(("group", "member")), P("group", "member", None))
    return jax.shard_map(
        local,
        mesh=mesh,
        in_specs=placed,
        out_specs=(P("group", "member", None), P("group", "member")),
        check_vma=False,
    )
```

time: 181 us -> 208 us (1.15)
  Pallas kernels: 103 us -> 121 us
  waiting for transfers between devices: 42.4 us -> 52.7 us
  other arithmetic: 7.25 us -> 0.48 us
  local copies, waits for them, and re-layouts: 2.3 us -> 8.26 us
    pallas_call x6, Pallas kernels: 85.5 us -> 109 us  [the longest x2 81.2 us: stats(): pl.pallas_call(functools.partial(stats_kernel, factor, step, tile, member...]
    ppermute x6, waiting for transfers between devices: 42.4 us -> 52.7 us  [rotate(): lax.ppermute(value, 'member', [(i, (i + step) % members) for i in range(m...]
    unnamed x8 -> x20, local copies, waits for them, and re-layouts: 2.3 us -> 8.26 us
    convert_element_type x3, other arithmetic: 3.98 us -> 0.25 us  [local(): partial = weigh(x, st, arrived[d], factor, tile, True).astype(jnp.float16)]
    convert_element_type x3, other arithmetic: 3.27 us -> 0.23 us  [local(): back.append(rotate(partial, -d).astype(jnp.float32))]
    pallas_call x1, Pallas kernels: 13.8 us -> 10.9 us  [regroup(): pl.pallas_call(regroup_kernel, out_shape=jax.ShapeDtypeStruct((clusters,...]
    pallas_call x1, Pallas kernels: 4.08 us -> 1.62 us  [finish(): pl.pallas_call(finish_kernel, out_shape=[jax.ShapeDtypeStruct((sub, dim),...]
  transfers between devices with their start and end apart: 7 -> 7, of which waited for: 3 -> 4; matrix products, arithmetic and copies ran while one was open for 3% -> 0% of each run, Pallas kernels for 34% -> 13%
where the time goes in v3:
time: 208 us
  Pallas kernels  121 us (58%)
  waiting for transfers between devices  52.7 us (25%)
  starting transfers between devices  24.3 us (12%)
  local copies, waits for them, and re-layouts  8.26 us (4%)
    pallas_call x2, Pallas kernels, stats(): pl.pallas_call(functools.partial(stats_kernel, factor, step, tile, member...  81.2 us
    ppermute x6, waiting for transfers between devices, rotate(): lax.ppermute(value, 'member', [(i, (i + step) % members) for i in range(m...  52.7 us
    pallas_call x4, Pallas kernels, weigh(): pl.pallas_call(functools.partial(weigh_kernel, factor, step, tile, send),...  27.3 us
    ppermute x6, starting transfers between devices, rotate(): lax.ppermute(value, 'member', [(i, (i + step) % members) for i in range(m...  19 us
    pallas_call x1, Pallas kernels, regroup(): pl.pallas_call(regroup_kernel, out_shape=jax.ShapeDtypeStruct((clusters,...  10.9 us
    unnamed x20, local copies, waits for them, and re-layouts  8.26 us
    all_to_all x1, starting transfers between devices, local(): x = lax.all_to_all(packed, 'group', split_axis=0, concat_axis=0, tiled=True)  5.33 us
  transfers between devices with their start and end apart: 7, of which 4 were waited for; matrix products, arithmetic and copies ran while one was open for 0% of the time, Pallas kernels for 13%

profile of v3, /device:TPU:0, one launch (start us, length us, event | category | flops | bytes accessed | tf_op | source)
XLA Modules:
  0.0 207.6 jit_solution(6332631513121271217)
XLA Ops:
  0.6 1.6 copy-done.2
  2.2 0.7 copy-done.9
  2.9 10.9 %regroup.1 = bf16[8,512,256]{2,1,0:T(8,128)(2,1)S(1)} custom-call(s32[32,128]{1,0:T(8,128)S(1)} %bitcast.17, bf16[4096,256]{1,0:T(8,128)(2,1)S(1)} %copy-done.2), custom_call_target="tpu_custom_call" | custom-call | flops 8589934592 | bytes 4194304 | tf_op jit(solution)/shard_map/regroup/pallas_call | solution.py:62
  13.8 1.3 copy-done
  15.2 5.3 %all-to-all-start = ((bf16[8,512,256]{2,1,0:T(8,128)(2,1)}), bf16[8,512,256]{2,1,0:T(8,128)(2,1)S(1)}, u32[]{:S(2)}, u32[]{:S(2)}) async-start(bf16[8,512,256]{2,1,0:T(8,128)(2,1)} %copy-done), calls=%async_computation | async-start | bytes 4194304 | tf_op jit(solution)/shard_map/all_to_all | solution.py:319
  20.5 1.6 collective-permute-start.2
  22.1 2.6 %collective-permute-start.1 = (bf16[1024,256]{1,0:T(8,128)(2,1)S(1)}, bf16[1024,256]{1,0:T(8,128)(2,1)S(1)}, u32[]{:S(2)}, u32[]{:S(2)}) collective-permute-start(bf16[1024,256]{1,0:T(8,128)(2,1)S(1)} %bitcast.11), channel_id=1, source_target_pairs={{0,2},{1,3},{2,0},{3,1},{4,6},{5,7},{6,4},{7,5},{8,10},{9,11},{10,... | collective-permute-start | bytes 1572872 | tf_op jit(solution)/shard_map/ppermute | solution.py:309
  24.7 1.3 collective-permute-start
  26.1 11.2 %collective-permute-done.2.refs_2_.refs_4_.c_ref = bf16[1024,256]{1,0:T(8,128)(2,1)S(1)} collective-permute-done((bf16[1024,256]{1,0:T(8,128)(2,1)S(1)}, bf16[1024,256]{1,0:T(8,128)(2,1)S(1)}, u32[]{:S(2)}, u32[]{:S(2)}) %collective-permute-start.2) | collective-permute-done | bytes 524320 | tf_op jit(solution)/shard_map/ppermute | solution.py:309
  37.3 0.8 copy-done.3
  38.1 21.2 %collective-permute-done.1.refs_1_.refs_3_.c_ref = bf16[1024,256]{1,0:T(8,128)(2,1)S(1)} collective-permute-done((bf16[1024,256]{1,0:T(8,128)(2,1)S(1)}, bf16[1024,256]{1,0:T(8,128)(2,1)S(1)}, u32[]{:S(2)}, u32[]{:S(2)}) %collective-permute-start.1) | collective-permute-done | bytes 524320 | tf_op jit(solution)/shard_map/ppermute | solution.py:309
  59.3 0.8 copy-done.6
  60.1 1.0 copy-done.4
  61.1 1.0 copy-done.7
  62.2 14.1 %stats.2.refs_1_ = f32[8,4096]{1,0:T(8,128)S(1)} custom-call(bf16[4096,256]{1,0:T(8,128)(2,1)S(1)} %bitcast.4, bf16[1024,256]{1,0:T(8,128)(2,1)S(1)} %bitcast.13, bf16[1024,256]{1,0:T(8,128)(2,1)S(1)} %copy-done.7, bf16[1024,256]{1,0:T(8,128)(2,1)S(1)} %copy-done.4), custom_call_target="tpu_custom_call" | custom-call | flops 6442450944 | bytes 3670016 | tf_op jit(solution)/shard_map/stats/pallas_call | solution.py:174
  76.3 67.1 %stats.3.st_ref = f32[8,4096]{1,0:T(8,128)S(1)} custom-call(bf16[4096,256]{1,0:T(8,128)(2,1)S(1)} %bitcast.5, bf16[1024,256]{1,0:T(8,128)(2,1)S(1)} %collective-permute-done.refs_0_.c_ref, f32[8,4096]{1,0:T(8,128)S(1)} %stats.2.refs_1_, bf16[1024,256]{1,0:T(8,128)(2,1)S(1)} %bitcast.14, bf16[1024,256]{1,0:T(8,128)(2,1)S(1)} %copy-done.7, ...), custom_call_target="tpu_custom_call" | custom-call | flops 2147483648 | bytes 2621440 | tf_op jit(solution)/shard_map/stats/pallas_call | solution.py:174
  143.4 6.9 %weigh.6 = f32[1040,256]{1,0:T(8,128)S(1)} custom-call(bf16[4096,256]{1,0:T(8,128)(2,1)S(1)} %bitcast.6, f32[8,4096]{1,0:T(8,128)S(1)} %stats.3.st_ref, bf16[1024,256]{1,0:T(8,128)(2,1)S(1)} %copy-done.5), custom_call_target="tpu_custom_call" | custom-call | flops 4294967296 | bytes 2621440 | tf_op jit(solution)/shard_map/weigh/pallas_call | solution.py:246
  150.4 0.9 copy-done.8
  151.3 6.9 %weigh.5 = f32[1040,256]{1,0:T(8,128)S(1)} custom-call(bf16[4096,256]{1,0:T(8,128)(2,1)S(1)} %bitcast.7, f32[8,4096]{1,0:T(8,128)S(1)} %stats.3.st_ref, bf16[1024,256]{1,0:T(8,128)(2,1)S(1)} %copy-done.8), custom_call_target="tpu_custom_call" | custom-call | flops 4294967296 | bytes 2621440 | tf_op jit(solution)/shard_map/weigh/pallas_call | solution.py:246
  158.4 12.8 %collective-permute-start.4 = (f16[1040,256]{1,0:T(8,128)(2,1)S(1)}, f16[1040,256]{1,0:T(8,128)(2,1)S(1)}, u32[]{:S(2)}, u32[]{:S(2)}) collective-permute-start(f16[1040,256]{1,0:T(8,128)(2,1)S(1)} %convert_element_type.20), channel_id=1, source_target_pairs={{0,3},{1,0},{2,1},{3,2},{4,7},{5,4},{6,5},{7,6},{8,11},{9,8},{10,9... | collective-permute-start | bytes 1597448 | tf_op jit(solution)/shard_map/ppermute | solution.py:309
  171.2 6.9 %weigh.7 = f32[1040,256]{1,0:T(8,128)S(1)} custom-call(bf16[4096,256]{1,0:T(8,128)(2,1)S(1)} %bitcast.8, f32[8,4096]{1,0:T(8,128)S(1)} %stats.3.st_ref, bf16[1024,256]{1,0:T(8,128)(2,1)S(1)} %collective-permute-done.refs_0_.c_ref), custom_call_target="tpu_custom_call" | custom-call | flops 4294967296 | bytes 2621440 | tf_op jit(solution)/shard_map/weigh/pallas_call | solution.py:246
  178.7 6.7 %weigh.4 = (f32[1024,256]{1,0:T(8,128)S(1)}, f32[1024,128]{1,0:T(8,128)S(1)}) custom-call(bf16[4096,256]{1,0:T(8,128)(2,1)S(1)} %bitcast.9, f32[8,4096]{1,0:T(8,128)S(1)} %stats.3.st_ref, bf16[1024,256]{1,0:T(8,128)(2,1)S(1)} %bitcast.15), custom_call_target="tpu_custom_call" | custom-call | flops 4294967296 | bytes 2621440 | tf_op jit(solution)/shard_map/weigh/pallas_call | solution.py:246
  185.8 20.1 %collective-permute-done.5 = f16[1040,256]{1,0:T(8,128)(2,1)S(1)} collective-permute-done((f16[1040,256]{1,0:T(8,128)(2,1)S(1)}, f16[1040,256]{1,0:T(8,128)(2,1)S(1)}, u32[]{:S(2)}, u32[]{:S(2)}) %collective-permute-start.5) | collective-permute-done | bytes 532512 | tf_op jit(solution)/shard_map/ppermute | solution.py:309
  206.0 1.6 finish.1
  (24 shorter events, 1.3 us)
Async XLA Ops:
  0.6 1.6 copy-start.2
  2.2 0.7 copy-start.9
  13.8 1.3 copy-start
  15.2 5.3 %copy-start.1 = (bf16[1,1024,256]{2,1,0:T(8,128)(2,1)S(1)}, bf16[1,1024,256]{2,1,0:T(8,128)(2,1)}, u32[]{:S(2)}) copy-start(bf16[1,1024,256]{2,1,0:T(8,128)(2,1)} %param.5) | copy-start | bytes 1572868
  15.2 44.9 %all-to-all-start = ((bf16[8,512,256]{2,1,0:T(8,128)(2,1)}), bf16[8,512,256]{2,1,0:T(8,128)(2,1)S(1)}, u32[]{:S(2)}, u32[]{:S(2)}) async-start(bf16[8,512,256]{2,1,0:T(8,128)(2,1)} %copy-done), calls=%async_computation | async-start | bytes 4194304 | tf_op jit(solution)/shard_map/all_to_all | solution.py:319
  20.5 16.8 %collective-permute-start.2 = (bf16[1024,256]{1,0:T(8,128)(2,1)S(1)}, bf16[1024,256]{1,0:T(8,128)(2,1)S(1)}, u32[]{:S(2)}, u32[]{:S(2)}) collective-permute-start(bf16[1024,256]{1,0:T(8,128)(2,1)S(1)} %bitcast.10), channel_id=1, source_target_pairs={{0,1},{1,2},{2,3},{3,0},{4,5},{5,6},{6,7},{7,4},{8,9},{9,10},{10,1... | collective-permute-start | bytes 1572872 | tf_op jit(solution)/shard_map/ppermute | solution.py:309
  22.1 37.1 %collective-permute-start.1 = (bf16[1024,256]{1,0:T(8,128)(2,1)S(1)}, bf16[1024,256]{1,0:T(8,128)(2,1)S(1)}, u32[]{:S(2)}, u32[]{:S(2)}) collective-permute-start(bf16[1024,256]{1,0:T(8,128)(2,1)S(1)} %bitcast.11), channel_id=1, source_target_pairs={{0,2},{1,3},{2,0},{3,1},{4,6},{5,7},{6,4},{7,5},{8,10},{9,11},{10,... | collective-permute-start | bytes 1572872 | tf_op jit(solution)/shard_map/ppermute | solution.py:309
  24.7 51.6 %collective-permute-start = (bf16[1024,256]{1,0:T(8,128)(2,1)S(1)}, bf16[1024,256]{1,0:T(8,128)(2,1)S(1)}, u32[]{:S(2)}, u32[]{:S(2)}) collective-permute-start(bf16[1024,256]{1,0:T(8,128)(2,1)S(1)} %bitcast.12), channel_id=1, source_target_pairs={{0,3},{1,0},{2,1},{3,2},{4,7},{5,4},{6,5},{7,6},{8,11},{9,8},{10,9... | collective-permute-start | bytes 1572872 | tf_op jit(solution)/shard_map/ppermute | solution.py:309
  37.3 0.8 copy-start.3
  59.3 0.8 copy-start.6
  60.1 1.0 copy-start.4
  61.1 1.0 copy-start.7
  76.3 67.1 %copy-start.5 = (bf16[1024,256]{1,0:T(8,128)(2,1)S(1)}, bf16[1024,256]{1,0:T(8,128)(2,1)}, u32[]{:S(2)}) copy-start(bf16[1024,256]{1,0:T(8,128)(2,1)} %copy-done.3) | copy-start | bytes 1572868
  150.3 1.0 copy-start.8
  158.3 27.3 %collective-permute-start.3 = (f16[1040,256]{1,0:T(8,128)(2,1)S(1)}, f16[1040,256]{1,0:T(8,128)(2,1)S(1)}, u32[]{:S(2)}, u32[]{:S(2)}) collective-permute-start(f16[1040,256]{1,0:T(8,128)(2,1)S(1)} %convert_element_type.18), channel_id=1, source_target_pairs={{0,2},{1,3},{2,0},{3,1},{4,6},{5,7},{6,4},{7,5},{8,10},{9,11},{10,... | collective-permute-start | bytes 1597448 | tf_op jit(solution)/shard_map/ppermute | solution.py:309
  158.4 27.4 %collective-permute-start.4 = (f16[1040,256]{1,0:T(8,128)(2,1)S(1)}, f16[1040,256]{1,0:T(8,128)(2,1)S(1)}, u32[]{:S(2)}, u32[]{:S(2)}) collective-permute-start(f16[1040,256]{1,0:T(8,128)(2,1)S(1)} %convert_element_type.20), channel_id=1, source_target_pairs={{0,3},{1,0},{2,1},{3,2},{4,7},{5,4},{6,5},{7,6},{8,11},{9,8},{10,9... | collective-permute-start | bytes 1597448 | tf_op jit(solution)/shard_map/ppermute | solution.py:309
  178.1 27.8 %collective-permute-start.5 = (f16[1040,256]{1,0:T(8,128)(2,1)S(1)}, f16[1040,256]{1,0:T(8,128)(2,1)S(1)}, u32[]{:S(2)}, u32[]{:S(2)}) collective-permute-start(f16[1040,256]{1,0:T(8,128)(2,1)S(1)} %convert_element_type.22), channel_id=1, source_target_pairs={{0,1},{1,2},{2,3},{3,0},{4,5},{5,6},{6,7},{7,4},{8,9},{9,10},{10,1... | collective-permute-start | bytes 1597448 | tf_op jit(solution)/shard_map/ppermute | solution.py:309
